TPU v7x, 256 devices: a whole 4x4x8 slice. The times are simulated.
256 devices in a mesh: bl: 64 (over y, z, core), ch: 4 (over x).
Axes of the slice: x: 4, y: 4, z: 8, core: 2. Of those that a mesh axis runs over, the one named last changes fastest.
Arguments:
- facet_grid: bfloat16 [4, 64, 16, 1024], P(None, None, None, 'ch'), may hold values from -0.75 to 0.75
- kernel: bfloat16 [131072, 1024], P('bl', 'ch'), may hold values from -0.1875 to 0.1875
- tile_of: int32 [256], P('bl'), may hold values from 0 to 3
- observed: bfloat16 [64, 2, 131072], P('ch', None, 'bl'), may hold values from -6 to 6
- flags: int32 [64, 131072], P('ch', 'bl'), may hold values 0 or 1
- pairs: int32 [2, 131072], P(None, 'bl'), may hold values from 0 to 511, as said below
- solver_order: int32 [512], replicated, may hold values from 0 to 511, as said below
Outputs:
- gains: float32 [64, 16, 512], P('ch', None, 'bl')
Inputs may be any that keep to these rules, and one draw needn't show every extreme that they name: `solver_order`: each station appears once. `pairs`: for row r, with j = (r mod 2048) // 32, the first station is solver_order[8 * j + m] for some m below 8; the second station differs from the first.
All inputs are finite; a program needn't handle non-finite values. No bound on the sum of `flags` on one device may be relied on, other than what follows from the above.
Results may differ from a plain program's by a relative error of at most 0.013.
Values may be sent and summed in bfloat16 or wider, within the bound.
No kernel may reach another device: no remote copies, remote signals or barrier semaphores. Data moves between devices by JAX's collectives and lax.ppermute only.
A program may use at most 128 MiB of HBM per device.

v0:
```python
import jax
import jax.numpy as jnp
from jax import lax
from jax.sharding import PartitionSpec as P

S = 512
ND = 8
ITERS = 4


def extended(shard, sides, width):
    for axis, dim in sides:
        devices, length = (lax.axis_size(axis), shard.shape[dim])
        up = [(i, (i + 1) % devices) for i in range(devices - 1)]
        down = [(j, i) for i, j in up]
        last = lax.slice_in_dim(shard, length - width, length, axis=dim)
        initial = lax.slice_in_dim(shard, 0, width, axis=dim)
        before = lax.ppermute(last, axis, up)
        after = lax.ppermute(initial, axis, down)
        shard = jnp.concatenate([before, shard, after], axis=dim)
    return shard


def lookup(gain_flat, pick):
    return jnp.dot(
        gain_flat, pick, precision=lax.Precision.HIGHEST, preferred_element_type=jnp.float32
    )


def row_terms(model_vis, visible, far_gain, near_gain):
    channels = model_vis.shape[0]
    row_count = model_vis.shape[2]
    model_pair = model_vis.reshape(channels, ND, 2, row_count)
    model_re = model_pair[:, :, 0].astype(jnp.float32)
    model_im = model_pair[:, :, 1].astype(jnp.float32)
    far_pair = far_gain.reshape(channels, ND, 2, row_count)
    near_pair = near_gain.reshape(channels, ND, 2, row_count)
    far_re = far_pair[:, :, 0]
    far_im = far_pair[:, :, 1]
    near_re = near_pair[:, :, 0]
    near_im = near_pair[:, :, 1]
    prod_re = model_re * far_re + model_im * far_im
    prod_im = model_im * far_re - model_re * far_im
    pred_re = jnp.sum(near_re * prod_re - near_im * prod_im, axis=1)
    pred_im = jnp.sum(near_re * prod_im + near_im * prod_re, axis=1)
    resid_re = visible[:, 0].astype(jnp.float32) - pred_re
    resid_im = visible[:, 1].astype(jnp.float32) - pred_im
    cross_re = prod_re * resid_re[:, None, :] + prod_im * resid_im[:, None, :]
    cross_im = prod_re * resid_im[:, None, :] - prod_im * resid_re[:, None, :]
    power = prod_re * prod_re + prod_im * prod_im
    stacked = jnp.concatenate([cross_re, cross_im, power], axis=1)
    return stacked.reshape(channels * 3 * ND, row_count)


def update_gains(gain_shard, sum_re, sum_im, power):
    channels = gain_shard.shape[0]
    owned = gain_shard.shape[2]
    gain_pair = gain_shard.reshape(channels, ND, 2, owned)
    gain_re = gain_pair[:, :, 0]
    gain_im = gain_pair[:, :, 1]
    new_re = (sum_re + gain_re * power) / (power + 1.0)
    new_im = (sum_im + gain_im * power) / (power + 1.0)
    averaged = jnp.stack([(gain_re + new_re) * 0.5, (gain_im + new_im) * 0.5], axis=2).reshape(
        channels, 2 * ND, owned
    )
    padded = extended(averaged, (("ch", 0),), 1)
    total_channels = channels * lax.axis_size("ch")
    chan_index = lax.axis_index("ch") * channels + jnp.arange(channels, dtype=jnp.int32)
    has_left = (chan_index > 0).astype(jnp.float32)[:, None, None]
    has_right = (chan_index < total_channels - 1).astype(jnp.float32)[:, None, None]
    return (0.25 * has_left * padded[:-2] + 0.5 * padded[1:-1] + 0.25 * has_right * padded[2:]) / (
        0.5 + 0.25 * has_left + 0.25 * has_right
    )


def body(facet_grid, kernel, tile_of, observed, flags, pairs, solver_order):
    channels = observed.shape[0]
    row_count = observed.shape[2]
    cell_count = kernel.shape[1]
    tile_count = facet_grid.shape[0]
    block_count = tile_of.shape[0]
    block_rows = row_count // block_count
    tile_pick = (tile_of[:, None] == jnp.arange(tile_count, dtype=jnp.int32)[None, :]).astype(
        jnp.bfloat16
    )
    kernel_blocks = kernel.reshape(block_count, block_rows, cell_count)
    chosen = jnp.einsum(
        "bt,tckg->bckg", tile_pick, facet_grid, preferred_element_type=jnp.float32
    ).astype(jnp.bfloat16)
    partial_vis = jnp.einsum(
        "bckg,bvg->ckbv", chosen, kernel_blocks, preferred_element_type=jnp.float32
    )
    summed = lax.psum_scatter(
        partial_vis.reshape(channels * lax.axis_size("ch"), partial_vis.shape[1], row_count).astype(
            jnp.bfloat16
        ),
        "ch",
        scatter_dimension=0,
        tiled=True,
    ).astype(jnp.float32)
    kept_rows = (1 - flags).astype(jnp.float32)
    model_vis = (summed * kept_rows[:, None, :]).astype(jnp.bfloat16)
    visible = (observed.astype(jnp.float32) * kept_rows[:, None, :]).astype(jnp.bfloat16)
    inverse = jnp.zeros((S,), jnp.int32).at[solver_order].set(jnp.arange(S, dtype=jnp.int32))
    bl_count = lax.axis_size("bl")
    owned = S // bl_count
    station_ids = jnp.arange(S, dtype=jnp.int32)[:, None]
    packed = pairs.reshape(1, 2, row_count)
    model_vis, visible, packed = (
        lax.all_to_all(model_vis, "bl", split_axis=2, concat_axis=2, tiled=True),
        lax.all_to_all(visible, "bl", split_axis=2, concat_axis=2, tiled=True),
        lax.all_to_all(packed, "bl", split_axis=2, concat_axis=2, tiled=True),
    )
    first_slot = inverse[packed[0, 0]]
    second_slot = inverse[packed[0, 1]]
    owner_slot = first_slot - lax.axis_index("bl") * owned
    near_pick = (owner_slot[None, :] == jnp.arange(owned, dtype=jnp.int32)[:, None]).astype(
        jnp.float32
    )
    far_pick = (second_slot[None, :] == station_ids).astype(jnp.float32)
    gain_shard = (
        jnp.zeros((channels, ND, 2, owned), jnp.float32)
        .at[:, :, 0, :]
        .set(1.0)
        .reshape(channels, 2 * ND, owned)
    )
    all_gains = (
        jnp.zeros((channels, ND, 2, S), jnp.float32)
        .at[:, :, 0, :]
        .set(1.0)
        .reshape(channels, 2 * ND, S)
    )
    for iteration in range(ITERS):
        if iteration > 0:
            all_gains = lax.all_gather(gain_shard, "bl", axis=2, tiled=True)
        far_gain = lookup(all_gains.reshape(channels * 2 * ND, S), far_pick)
        near_gain = lookup(gain_shard.reshape(channels * 2 * ND, owned), near_pick)
        stacked = row_terms(model_vis, visible, far_gain, near_gain)
        station_terms = jnp.einsum(
            "fv,sv->fs",
            stacked,
            near_pick,
            precision=lax.Precision.HIGHEST,
            preferred_element_type=jnp.float32,
        )
        mine = station_terms.reshape(channels, 3 * ND, owned)
        sum_re = mine[:, :ND]
        sum_im = mine[:, ND : 2 * ND]
        sum_power = mine[:, 2 * ND :]
        gain_shard = update_gains(gain_shard, sum_re, sum_im, sum_power)
    return gain_shard


def solution(mesh):
    in_specs = (
        P(None, None, None, "ch"),
        P("bl", "ch"),
        P("bl"),
        P("ch", None, "bl"),
        P("ch", "bl"),
        P(None, "bl"),
        P(),
    )
    out_specs = P("ch", None, "bl")
    return jax.shard_map(body, mesh=mesh, in_specs=in_specs, out_specs=out_specs, check_vma=False)
```

profile of v0, /device:TPU:1, one launch (start us, length us, event | category | flops | bytes accessed | tf_op | source)
XLA Modules:
  0.0 517.9 jit_solution(18245494994774000052)
XLA Ops:
  6.5 1.6 copy-done
  8.1 2.4 fusion.41
  11.9 2.6 copy.212
  16.5 13.1 %all-to-all-start.1 = ((s32[1,2,2048]{1,0,2:T(1,128)}), s32[1,2,2048]{1,0,2:T(1,128)S(1)}, u32[]{:S(2)}, u32[]{:S(2)}) async-start(s32[1,2,2048]{1,0,2:T(1,128)} %bitcast.7), calls=%async_computation.2 | async-start | bytes 2097152 | tf_op jit(solution)/shard_map/all_to_all | solution.py:112
  30.7 1.8 reshape.311
  32.5 2.4 scatter_custom_fusion
  35.0 23.2 %all-to-all-done.1 = s32[1,2,2048]{1,0,2:T(1,128)S(1)} async-done(((s32[1,2,2048]{1,0,2:T(1,128)}), s32[1,2,2048]{1,0,2:T(1,128)S(1)}, u32[]{:S(2)}, u32[]{:S(2)}) %all-to-all-start.1) | async-done | bytes 16416 | tf_op jit(solution)/shard_map/all_to_all | solution.py:112
  58.2 6.2 %all-to-all-start.2 = ((bf16[64,2,512]{2,1,0:T(2,128)(2,1)}), bf16[64,2,512]{2,1,0:T(2,128)(2,1)S(1)}, u32[]{:S(2)}, u32[]{:S(2)}) async-start(bf16[64,2,512]{2,1,0:T(2,128)(2,1)} %reshape.311), calls=%async_computation.3 | async-start | bytes 262144 | tf_op jit(solution)/shard_map/all_to_all | solution.py:111
  64.4 106.4 %slice_reduce_fusion = (s32[2048]{0:T(1024)S(1)}, s32[2048]{0:T(1024)S(1)}) fusion(s32[1,2,2048]{1,0,2:T(1,128)S(1)} %all-to-all-done.1), kind=kLoop, calls=%fused_computation.86 | loop fusion | bytes 32768 | tf_op jit(solution)/shard_map/slice | solution.py:114
  170.9 1.5 multiply_convert_fusion
  172.4 8.6 %copy.107 = bf16[16,16,2048]{1,0,2:T(8,128)(2,1)} copy(bf16[16,16,2048]{2,1,0:T(8,128)(2,1)S(1)} %multiply_convert_fusion) | data formatting | bytes 2097152 | tf_op jit(solution)/shard_map/convert_element_type | solution.py:102
  181.0 12.5 %reshape.309 = bf16[64,2,4096]{2,1,0:T(2,128)(2,1)} reshape(bf16[2048,16,16]{2,1,0:T(8,128)(2,1)} %bitcast.247) | data formatting | bytes 2097152
  193.4 10.7 %all-to-all-start = ((bf16[64,2,4096]{2,1,0:T(2,128)(2,1)}), bf16[64,2,4096]{2,1,0:T(2,128)(2,1)S(1)}, u32[]{:S(2)}, u32[]{:S(2)}) async-start(bf16[64,2,4096]{2,1,0:T(2,128)(2,1)} %reshape.309), calls=%async_computation.1 | async-start | bytes 2097152 | tf_op jit(solution)/shard_map/all_to_all | solution.py:110
  204.1 13.2 %gather_fusion.1 = s32[2048]{0:T(1024)S(1)} fusion(s32[512]{0:T(512)S(1)} %scatter_custom_fusion, s32[2048]{0:T(1024)S(1)} %broadcast_clamp_fusion), kind=kCustom, calls=%fused_computation.1 | custom fusion | bytes 24576 | tf_op jit(solution)/shard_map/gather | solution.py:114
  217.4 13.2 %gather_fusion = s32[2048]{0:T(1024)S(1)} fusion(s32[512]{0:T(512)S(1)} %scatter_custom_fusion, s32[2048]{0:T(1024)S(1)} %broadcast_clamp_fusion.1), kind=kCustom, calls=%fused_computation | custom fusion | bytes 24576 | tf_op jit(solution)/shard_map/gather | solution.py:115
  230.7 2.4 fusion.129
  233.0 3.4 fusion.8
  237.1 2.3 fusion.168
  239.4 2.2 copy.203
  242.2 7.6 %reshape.310 = bf16[2048,16,16]{2,1,0:T(8,128)(2,1)} reshape(bf16[64,2,4096]{2,1,0:T(2,128)(2,1)S(1)} %all-to-all-done) | data formatting | bytes 2097152
  249.8 9.1 %copy.108 = bf16[16,16,2048]{2,0,1:T(8,128)(2,1)S(1)} copy(bf16[16,16,2048]{1,0,2:T(8,128)(2,1)} %bitcast.248) | data formatting | bytes 2097152 | tf_op jit(solution)/shard_map/all_to_all | solution.py:110
  259.0 1.5 copy-done.2
  260.5 2.9 subtract_reduce_fusion.3
  264.0 3.9 fusion.10
  269.7 4.0 collective-permute-start
  274.7 56.0 %all_gather.9 = f32[16,16,512]{0,2,1:T(8,128)} all-gather(f32[16,16,8]{0,2,1:T(8,128)S(1)} %fusion.111), channel_id=1, replica_groups=mesh['bl'=64,'ch'=4] {'bl'}, dimensions={2}, use_global_device_ids=true | all-gather | bytes 532480 | tf_op jit(solution)/shard_map/all_gather | solution.py:135
  331.5 2.9 copy.176
  334.4 2.1 fusion.4
  338.9 1.5 copy.205
  340.4 1.5 copy.206
  342.3 3.9 fusion.16
  346.7 3.6 collective-permute-start.2
  352.0 3.6 collective-permute-done.3
  355.7 53.5 %all_gather.10 = f32[16,16,512]{0,2,1:T(8,128)} all-gather(f32[16,16,8]{0,2,1:T(8,128)S(1)} %fusion.98), channel_id=1, replica_groups=mesh['bl'=64,'ch'=4] {'bl'}, dimensions={2}, use_global_device_ids=true | all-gather | bytes 532480 | tf_op jit(solution)/shard_map/all_gather | solution.py:135
  410.0 2.9 copy.180
  412.9 2.1 fusion.2
  418.8 1.5 copy.208
  420.8 3.9 fusion.22
  425.1 3.1 collective-permute-start.4
  430.0 3.6 collective-permute-done.5
  433.6 53.5 %all_gather.11 = f32[16,16,512]{0,2,1:T(8,128)} all-gather(f32[16,16,8]{0,2,1:T(8,128)S(1)} %fusion.85), channel_id=1, replica_groups=mesh['bl'=64,'ch'=4] {'bl'}, dimensions={2}, use_global_device_ids=true | all-gather | bytes 532480 | tf_op jit(solution)/shard_map/all_gather | solution.py:135
  487.2 2.9 copy.184
  490.1 2.1 fusion.6
  493.2 1.9 subtract_reduce_fusion
  495.4 1.8 multiply_add_fusion.1
  497.2 3.9 fusion.28
  501.6 3.1 collective-permute-start.6
  506.4 3.6 collective-permute-done.7
  (132 shorter events, 26.1 us)
Async XLA Ops:
  6.5 1.6 copy-start
  6.5 4.0 copy-start.3
  6.5 164.3 %reduce-scatter.2.cloned.1.call-start = ((), (), s32[]{:S(2)}) async-start(), calls=%async_computation.4 | async-start | bytes 5242880 | tf_op jit(solution)/shard_map/reduce_scatter | solution.py:93
  14.5 0.7 copy-start.11
  14.5 15.2 %copy-start.19 = (s32[512]{0:T(512)S(1)}, s32[512]{0:T(512)}, u32[]{:S(2)}) copy-start(s32[512]{0:T(512)} %param.17) | copy-start | bytes 6148
  14.5 15.3 %copy-start.10 = (s32[16,2048]{1,0:T(8,128)S(1)}, s32[16,2048]{1,0:T(8,128)}, u32[]{:S(2)}) copy-start(s32[16,2048]{1,0:T(8,128)} %param.15) | copy-start | bytes 393220
  14.5 15.3 %copy-start.8 = (bf16[16,2,2048]{2,1,0:T(2,128)(2,1)S(1)}, bf16[16,2,2048]{2,1,0:T(2,128)(2,1)}, u32[]{:S(2)}) copy-start(bf16[16,2,2048]{2,1,0:T(2,128)(2,1)} %param.14) | copy-start | bytes 393220
  16.5 41.7 %all-to-all-start.1 = ((s32[1,2,2048]{1,0,2:T(1,128)}), s32[1,2,2048]{1,0,2:T(1,128)S(1)}, u32[]{:S(2)}, u32[]{:S(2)}) async-start(s32[1,2,2048]{1,0,2:T(1,128)} %bitcast.7), calls=%async_computation.2 | async-start | bytes 2097152 | tf_op jit(solution)/shard_map/all_to_all | solution.py:112
  29.9 244.7 %copy-start.12 = (f32[16]{0:T(128)}, f32[16]{0:T(128)S(1)}, u32[]{:S(2)}) copy-start(f32[16]{0:T(128)S(1)} %add_add_fusion) | copy-start | bytes 196
  58.2 135.2 %all-to-all-start.2 = ((bf16[64,2,512]{2,1,0:T(2,128)(2,1)}), bf16[64,2,512]{2,1,0:T(2,128)(2,1)S(1)}, u32[]{:S(2)}, u32[]{:S(2)}) async-start(bf16[64,2,512]{2,1,0:T(2,128)(2,1)} %reshape.311), calls=%async_computation.3 | async-start | bytes 262144 | tf_op jit(solution)/shard_map/all_to_all | solution.py:111
  193.4 48.7 %all-to-all-start = ((bf16[64,2,4096]{2,1,0:T(2,128)(2,1)}), bf16[64,2,4096]{2,1,0:T(2,128)(2,1)S(1)}, u32[]{:S(2)}, u32[]{:S(2)}) async-start(bf16[64,2,4096]{2,1,0:T(2,128)(2,1)} %reshape.309), calls=%async_computation.1 | async-start | bytes 2097152 | tf_op jit(solution)/shard_map/all_to_all | solution.py:110
  217.4 13.3 %copy-start.9 = (f32[16,8,2,8]{3,1,0,2:T(8,128)S(1)}, f32[16,8,2,8]{3,1,0,2:T(8,128)}, u32[]{:S(2)}) copy-start(f32[16,8,2,8]{3,1,0,2:T(8,128)} %constant.98) | copy-start | bytes 24580
  217.4 15.6 %copy-start.20 = (f32[16,8,2,512]{3,1,2,0:T(8,128)S(1)}, f32[16,8,2,512]{3,1,2,0:T(8,128)}, u32[]{:S(2)}) copy-start(f32[16,8,2,512]{3,1,2,0:T(8,128)} %constant.89.clone.1) | copy-start | bytes 1572868
  230.6 103.8 %copy-start.16 = (s32[2048]{0:T(1024)}, s32[2048]{0:T(1024)S(1)}, u32[]{:S(2)}) copy-start(s32[2048]{0:T(1024)S(1)} %gather_fusion) | copy-start | bytes 24580
  258.9 1.6 copy-start.2
  268.3 6.3 %collective-permute-start.1 = (f32[1,16,8]{0,2,1:T(8,128)S(1)}, f32[1,16,8]{0,2,1:T(8,128)S(1)}, u32[]{:S(2)}, u32[]{:S(2)}) collective-permute-start(f32[1,16,8]{0,2,1:T(8,128)S(1)} %copy.127), channel_id=1, source_target_pairs={{1,0},{2,1},{3,2},{5,4},{6,5},{7,6},{9,8},{10,9},{11,10},{13,12},{... | collective-permute-start | bytes 1544 | tf_op jit(solution)/shard_map/ppermute | solution.py:19
  269.7 4.8 collective-permute-start
  342.3 4.0 copy-start.4
  342.3 4.0 copy-start.6
  342.3 13.2 %copy-start.13 = (f32[16]{0:T(128)S(1)}, f32[16]{0:T(128)}, u32[]{:S(2)}) copy-start(f32[16]{0:T(128)} %copy-done.12) | copy-start | bytes 196
  346.7 5.3 %collective-permute-start.2 = (f32[1,16,8]{0,2,1:T(8,128)S(1)}, f32[1,16,8]{0,2,1:T(8,128)S(1)}, u32[]{:S(2)}, u32[]{:S(2)}) collective-permute-start(f32[1,16,8]{0,2,1:T(8,128)S(1)} %copy.138), channel_id=1, source_target_pairs={{0,1},{1,2},{2,3},{4,5},{5,6},{6,7},{8,9},{9,10},{10,11},{12,13},{... | collective-permute-start | bytes 1544 | tf_op jit(solution)/shard_map/ppermute | solution.py:18
  350.6 5.0 collective-permute-start.3
  409.2 3.6 copy-start.17
  420.7 4.0 copy-start.5
  420.8 4.0 copy-start.7
  420.8 12.7 %copy-start.14 = (f32[16]{0:T(128)S(1)}, f32[16]{0:T(128)}, u32[]{:S(2)}) copy-start(f32[16]{0:T(128)} %copy-done.12) | copy-start | bytes 196
  425.1 4.8 collective-permute-start.4
  428.5 5.0 collective-permute-start.5
  487.1 3.0 copy-start.18
  495.4 15.4 %copy-start.1 = (bf16[4,64,16,256]{3,2,1,0:T(8,128)(2,1)S(1)}, bf16[4,64,16,256]{3,2,1,0:T(8,128)(2,1)}, u32[]{:S(2)}) copy-start(bf16[4,64,16,256]{3,2,1,0:T(8,128)(2,1)} %param.11) | copy-start | bytes 6291460
  497.2 12.7 %copy-start.15 = (f32[16]{0:T(128)S(1)}, f32[16]{0:T(128)}, u32[]{:S(2)}) copy-start(f32[16]{0:T(128)} %copy-done.12) | copy-start | bytes 196
  501.6 4.8 collective-permute-start.6
  504.9 5.0 collective-permute-start.7
Sparse Core Ops, SparseCore 0:
  14.6 53.0 reduce-scatter.1
where the time goes:
time: 525 us; the launch traced here: 518 us
  local copies, waits for them, and re-layouts  209 us (40%)
  blocking collectives  163 us (31%)
  starting transfers between devices  49 us (9%)
  waiting for transfers between devices  34.6 us (7%)
  matrix products  34.3 us (7%)
  between operations  14.5 us (3%)
  other arithmetic  13.8 us (3%)
    all_gather x3, blocking collectives, body(): all_gains = lax.all_gather(gain_shard, 'bl', axis=2, tiled=True)  163 us
    slice x1, local copies, waits for them, and re-layouts, body(): first_slot = inverse[packed[0, 0]]  106 us
    unnamed x55, local copies, waits for them, and re-layouts  36.5 us
    all_to_all x1, waiting for transfers between devices, body(): lax.all_to_all(packed, 'bl', split_axis=2, concat_axis=2, tiled=True)  23.2 us
    dot_general x4, matrix products, body(): jnp.einsum('fv,sv->fs', stacked, near_pick, precision=lax.Precision.HIGHE...  15.8 us
    dot_general x8, matrix products, lookup(): jnp.dot(gain_flat, pick, precision=lax.Precision.HIGHEST, preferred_eleme...  14.9 us
    ppermute x4, starting transfers between devices, extended(): before = lax.ppermute(last, axis, up)  13.8 us
    gather x1, local copies, waits for them, and re-layouts, body(): first_slot = inverse[packed[0, 0]]  13.2 us
  transfers between devices with their start and end apart: 12, of which 5 were waited for; matrix products, arithmetic and copies ran while one was open for 34% of the time, Pallas kernels for 0%

commit v1 on v0

v1 whole, which is shorter than its diff:
```python
import jax
import jax.numpy as jnp
from jax import lax
from jax.experimental import pallas as pl
from jax.experimental.pallas import tpu as pltpu
from jax.sharding import PartitionSpec as P

S = 512
ND = 8
ITERS = 4
LANES = 128
ROWS = 2048
HALF = 1024
BLK = 512
CHUNK = 256
F32 = jnp.float32
BF16 = jnp.bfloat16


def nt(a, b):
    return lax.dot_general(a, b, (((1,), (1,)), ((), ())), preferred_element_type=F32)


def nn(a, b):
    return lax.dot_general(a, b, (((1,), (0,)), ((), ())), preferred_element_type=F32)


def iota(shape, dim):
    return lax.broadcasted_iota(jnp.int32, shape, dim)


def lane_order():
    lane = iota((256, 256), 0)
    source = (lane & 15) * 16 + ((lane >> 4) & 7) * 2 + (lane >> 7)
    return (iota((256, 256), 1) == source).astype(F32).astype(BF16)


def degrid_kernel(groups):
    def run(where_ref, tile_ref, kern_ref, facet_ref, *outs):
        order = lane_order()
        here = where_ref[0]
        for block in range(4):
            rows = kern_ref[block * BLK : (block + 1) * BLK, :]
            tile = tile_ref[block]
            for index, shift in enumerate(groups):
                first = ((here + shift) & 3) * 16
                facet = facet_ref[tile, pl.ds(first, 16)].reshape(256, 256)
                facet = nn(order, facet).astype(BF16)
                out = outs[2 * index + block // 2]
                start = (block % 2) * BLK
                out[start : start + BLK, :] = nt(rows, facet).astype(BF16)

    return run


def degrid(where, tile_of, kernel, facet_grid, groups):
    smem = pl.BlockSpec(memory_space=pltpu.SMEM)
    vmem = pl.BlockSpec(memory_space=pltpu.VMEM)
    return pl.pallas_call(
        degrid_kernel(groups),
        out_shape=[jax.ShapeDtypeStruct((HALF, 256), BF16)] * (2 * len(groups)),
        in_specs=[smem, smem, vmem, vmem],
        out_specs=[vmem] * (2 * len(groups)),
        name="degrid%d" % len(groups),
    )(where, tile_of, kernel, facet_grid)


def payload_kernel(obs_ref, flag_ref, pair_ref, out_ref):
    kept = (1 - flag_ref[...]).astype(F32)
    pair = pair_ref[...]
    high = (pair >> 3).astype(F32)
    low = (pair & 7).astype(F32)
    fill = jnp.zeros((LANES - 52, ROWS), F32)
    stacked = jnp.concatenate([obs_ref[...].astype(F32), kept, high, low, fill], axis=0)
    for part in range(ROWS // 128):
        out_ref[part * 128 : (part + 1) * 128, :] = stacked[:, part * 128 : (part + 1) * 128].T.astype(BF16)


def make_payload(observed, flags, pairs):
    return pl.pallas_call(
        payload_kernel,
        out_shape=jax.ShapeDtypeStruct((ROWS, LANES), BF16),
        name="payload",
    )(observed.reshape(32, ROWS), flags, pairs)


def setup_kernel(pay_ref, order_ref, own_ref, ohq_ref, ohp_ref, opt_ref, vre_ref, vim_ref, kept_ref):
    source = iota((LANES, 5 * LANES), 0)
    col = iota((LANES, 5 * LANES), 1)
    piece = col >> 7
    chan = col & 15
    spread = (source == 2 * chan + piece) & (piece < 2)
    spread = spread | ((source == 32 + chan) & (piece == 2))
    weight = spread.astype(F32)
    weight = weight + 8.0 * ((source == 49) & (piece == 3)).astype(F32) + ((source == 51) & (piece == 3)).astype(F32)
    weight = weight + 8.0 * ((source == 48) & (piece == 4)).astype(F32) + ((source == 50) & (piece == 4)).astype(F32)
    weight = weight.astype(BF16)
    order = order_ref[...]
    own = own_ref[...]

    def step(i, carry):
        rows = pl.ds(pl.multiple_of(i * CHUNK, CHUNK), CHUNK)
        wide = nn(pay_ref[rows, :], weight)
        kept = wide[:, 256:384]
        vre_ref[rows, :] = wide[:, :128] * kept
        vim_ref[rows, :] = wide[:, 128:256] * kept
        kept_ref[rows, :] = kept
        second = wide[:, 384:512]
        first = wide[:, 512:640]
        for part in range(4):
            lanes = slice(part * 128, (part + 1) * 128)
            ohq_ref[rows, lanes] = (second == order[:, lanes]).astype(F32).astype(BF16)
        near = (first == own).astype(F32)
        ohp_ref[rows, :] = near.astype(BF16)
        opt_ref[:, rows] = near.T[:16, :].astype(BF16)
        return carry

    lax.fori_loop(0, ROWS // CHUNK, step, 0)


def make_setup(payload, order, own):
    shapes = [
        jax.ShapeDtypeStruct((ROWS, S), BF16),
        jax.ShapeDtypeStruct((ROWS, LANES), BF16),
        jax.ShapeDtypeStruct((16, ROWS), BF16),
        jax.ShapeDtypeStruct((ROWS, LANES), F32),
        jax.ShapeDtypeStruct((ROWS, LANES), F32),
        jax.ShapeDtypeStruct((ROWS, LANES), F32),
    ]
    return pl.pallas_call(setup_kernel, out_shape=shapes, name="setup")(payload, order, own)


def over_directions(x):
    x = x + pltpu.roll(x, 16, 1)
    x = x + pltpu.roll(x, 32, 1)
    return x + pltpu.roll(x, 64, 1)


def iterate_kernel(first):
    def run(*refs):
        if first:
            model_ref, opt_ref, vre_ref, vim_ref, kept_ref, out_ref = refs
        else:
            model_ref, opt_ref, vre_ref, vim_ref, kept_ref, ohq_ref, ohp_ref, all_ref, own_ref, out_ref = refs
            all_gains = all_ref[...]
            own = own_ref[...]
            high = own.astype(BF16).astype(F32)
            near_gains = jnp.concatenate([high, own - high, jnp.zeros((LANES - 16, 256), F32)], axis=0).astype(BF16)

        def step(i, acc):
            rows = pl.ds(pl.multiple_of(i * CHUNK, CHUNK), CHUNK)
            kept = kept_ref[rows, :]
            model_re = model_ref[rows, :128].astype(F32) * kept
            model_im = model_ref[rows, 128:].astype(F32) * kept
            if first:
                prod_re = pred_re = model_re
                prod_im = pred_im = model_im
            else:
                far = nn(ohq_ref[rows, :], all_gains)
                near = nn(ohp_ref[rows, :], near_gains)
                far_re, far_im = far[:, :128], far[:, 128:]
                near_re, near_im = near[:, :128], near[:, 128:]
                prod_re = model_re * far_re + model_im * far_im
                prod_im = model_im * far_re - model_re * far_im
                pred_re = near_re * prod_re - near_im * prod_im
                pred_im = near_re * prod_im + near_im * prod_re
            res_re = vre_ref[rows, :] - over_directions(pred_re)
            res_im = vim_ref[rows, :] - over_directions(pred_im)
            terms = jnp.concatenate(
                [
                    prod_re * res_re + prod_im * res_im,
                    prod_re * res_im - prod_im * res_re,
                    prod_re * prod_re + prod_im * prod_im,
                ],
                axis=1,
            )
            top = terms.astype(BF16)
            rest = (terms - top.astype(F32)).astype(BF16)
            pick = opt_ref[:, rows]
            return acc + nn(pick, top) + nn(pick, rest)

        acc = lax.fori_loop(0, ROWS // CHUNK, step, jnp.zeros((16, 384), F32))[:8]
        sum_re, sum_im, power = acc[:, :128], acc[:, 128:256], acc[:, 256:]
        if first:
            gain_re = jnp.ones((8, 128), F32)
            gain_im = jnp.zeros((8, 128), F32)
        else:
            gain_re, gain_im = own[:, :128], own[:, 128:]
        new_re = (sum_re + gain_re * power) / (power + 1.0)
        new_im = (sum_im + gain_im * power) / (power + 1.0)
        out_ref[:, :128] = (gain_re + new_re) * 0.5
        out_ref[:, 128:] = (gain_im + new_im) * 0.5

    return run


def iterate(args, first):
    return pl.pallas_call(
        iterate_kernel(first),
        out_shape=jax.ShapeDtypeStruct((8, 256), F32),
        name="iterate0" if first else "iterate",
    )(*args)


def smooth_kernel(spread):
    def run(where_ref, mid_ref, low_ref, high_ref, out_ref, *more):
        chan = iota((8, LANES), 1) & 15
        whole = chan + 16 * where_ref[0]
        has_left = (whole > 0).astype(F32)
        has_right = (whole < 63).astype(F32)
        for part in range(2):
            lanes = slice(part * 128, (part + 1) * 128)
            mid = mid_ref[:, lanes]
            left = jnp.where(chan == 0, pltpu.roll(low_ref[:, lanes], 113, 1), pltpu.roll(mid, 1, 1))
            right = jnp.where(chan == 15, pltpu.roll(high_ref[:, lanes], 15, 1), pltpu.roll(mid, 127, 1))
            total = 0.25 * has_left * left + 0.5 * mid + 0.25 * has_right * right
            out_ref[:, lanes] = total / (0.5 + 0.25 * has_left + 0.25 * has_right)
        if spread:
            more[0][...] = jnp.broadcast_to(out_ref[...].astype(BF16)[None], (64, 8, 256))

    return run


def smooth(where, mid, low, high, spread):
    shapes = [jax.ShapeDtypeStruct((8, 256), F32)]
    if spread:
        shapes.append(jax.ShapeDtypeStruct((64, 8, 256), BF16))
    smem = pl.BlockSpec(memory_space=pltpu.SMEM)
    vmem = pl.BlockSpec(memory_space=pltpu.VMEM)
    return pl.pallas_call(
        smooth_kernel(spread),
        out_shape=shapes,
        in_specs=[smem, vmem, vmem, vmem],
        out_specs=[vmem] * len(shapes),
        name="smooth",
    )(where, mid, low, high)


def add_kernel(own_a, own_b, chain_a, chain_b, near_a, near_b, out_ref):
    out_ref[:HALF, :] = (own_a[...].astype(F32) + chain_a[...].astype(F32) + near_a[...].astype(F32)).astype(BF16)
    out_ref[HALF:, :] = (own_b[...].astype(F32) + chain_b[...].astype(F32) + near_b[...].astype(F32)).astype(BF16)


def body(facet_grid, kernel, tile_of, observed, flags, pairs, solver_order):
    where = lax.axis_index("ch").astype(jnp.int32).reshape(1)
    up = [(i, (i + 1) % 4) for i in range(4)]
    down = [(i, (i + 3) % 4) for i in range(4)]

    far_a, far_b = degrid(where, tile_of, kernel, facet_grid, (2,))
    chain_a = lax.ppermute(far_a, "ch", up)
    chain_b = lax.ppermute(far_b, "ch", down)
    next_a, next_b, prev_a, prev_b, own_a, own_b = degrid(where, tile_of, kernel, facet_grid, (1, 3, 0))
    direct_a = lax.ppermute(prev_a, "ch", down)
    direct_b = lax.ppermute(next_b, "ch", up)
    chain_a = lax.ppermute((chain_a.astype(F32) + next_a.astype(F32)).astype(BF16), "ch", up)
    chain_b = lax.ppermute((chain_b.astype(F32) + prev_b.astype(F32)).astype(BF16), "ch", down)

    payload = make_payload(observed, flags, pairs).reshape(64, 32, LANES)
    payload = lax.all_to_all(payload, "bl", split_axis=0, concat_axis=0, tiled=True)
    mine = lax.dynamic_slice(solver_order, (8 * lax.axis_index("bl"),), (8,))
    own_row = jnp.concatenate([mine, mine, jnp.full((LANES - 16,), -1, jnp.int32)]).astype(F32).reshape(1, LANES)
    order_row = solver_order.astype(F32).reshape(1, S)
    ohq, ohp, opt, vis_re, vis_im, kept = make_setup(payload.reshape(ROWS, LANES), order_row, own_row)

    model = pl.pallas_call(
        add_kernel, out_shape=jax.ShapeDtypeStruct((ROWS, 256), BF16), name="add"
    )(own_a, own_b, chain_a, chain_b, direct_a, direct_b)
    model = lax.all_to_all(model.reshape(64, 32, 256), "bl", split_axis=0, concat_axis=0, tiled=True)
    common = (model.reshape(ROWS, 256), opt, vis_re, vis_im, kept)

    for step in range(ITERS):
        if step == 0:
            mid = iterate(common, True)
        else:
            mid = iterate(common + (ohq, ohp, everyone.reshape(S, 256), gains), False)
        low = lax.ppermute(mid, "ch", up)
        high = lax.ppermute(mid, "ch", down)
        if step + 1 < ITERS:
            gains, block = smooth(where, mid, low, high, True)
            everyone = lax.all_to_all(block, "bl", split_axis=0, concat_axis=0, tiled=True)
        else:
            (gains,) = smooth(where, mid, low, high, False)
    return gains.reshape(8, 2, ND, 16).transpose(3, 2, 1, 0).reshape(16, 2 * ND, 8)


def solution(mesh):
    in_specs = (
        P(None, None, None, "ch"),
        P("bl", "ch"),
        P("bl"),
        P("ch", None, "bl"),
        P("ch", "bl"),
        P(None, "bl"),
        P(),
    )
    out_specs = P("ch", None, "bl")
    return jax.shard_map(body, mesh=mesh, in_specs=in_specs, out_specs=out_specs, check_vma=False)
```

time: 525 us -> 221 us (0.42); the launches traced: 518 us -> 219 us
  local copies, waits for them, and re-layouts: 209 us -> 6.68 us
  blocking collectives: 163 us -> 58.6 us
  Pallas kernels: 0 us -> 60.5 us
  matrix products: 34.3 us -> 0 us
  waiting for transfers between devices: 34.6 us -> 51.9 us
  between operations: 14.5 us -> 0.12 us
  starting transfers between devices: 49 us -> 38 us
  other arithmetic: 13.8 us -> 3.6 us
    all_gather x3 -> x0, blocking collectives: 163 us -> none  [body(): all_gains = lax.all_gather(gain_shard, 'bl', axis=2, tiled=True)]
    slice x21 -> x0, local copies, waits for them, and re-layouts: 112 us -> none  [the longest x1 106 us: body(): first_slot = inverse[packed[0, 0]]]
    pallas_call x0 -> x13, Pallas kernels: none -> 60.5 us  [the longest x4 34.4 us: iterate(): pl.pallas_call(iterate_kernel(first), out_shape=jax.ShapeDtypeStruct((8,...]
    all_to_all x0 -> x3, blocking collectives: none -> 58.6 us  [body(): lax.all_to_all(block, 'bl', split_axis=0, concat_axis=0, tiled=True)]
    dot_general x14 -> x0, matrix products: 34.3 us -> none  [the longest x4 15.8 us: body(): jnp.einsum('fv,sv->fs', stacked, near_pick, precision=lax.Precision.HIGHE...]
    unnamed x55 -> x32, local copies, waits for them, and re-layouts: 36.5 us -> 4.38 us
    gather x2 -> x0, local copies, waits for them, and re-layouts: 26.4 us -> none  [the longest x1 13.2 us: body(): first_slot = inverse[packed[0, 0]]]
    ppermute x8 -> x14, waiting for transfers between devices: 11.3 us -> 30.8 us  [the longest x1 11.2 us: body(): lax.ppermute((chain_a.astype(F32) + next_a.astype(F32)).astype(BF16), 'ch...]
  transfers between devices with their start and end apart: 12 -> 16, of which waited for: 5 -> 12; matrix products, arithmetic and copies ran while one was open for 34% -> 2% of each run, Pallas kernels for 0% -> 8%
where the time goes in v1:
time: 221 us; the launch traced here: 219 us
  Pallas kernels  60.5 us (27%)
  blocking collectives  58.6 us (27%)
  waiting for transfers between devices  51.9 us (23%)
  starting transfers between devices  38 us (17%)
  local copies, waits for them, and re-layouts  6.68 us (3%)
  other arithmetic  3.6 us (2%)
    all_to_all x3, blocking collectives, body(): lax.all_to_all(block, 'bl', split_axis=0, concat_axis=0, tiled=True)  58.6 us
    pallas_call x4, Pallas kernels, iterate(): pl.pallas_call(iterate_kernel(first), out_shape=jax.ShapeDtypeStruct((8,...  34.4 us
    all_to_all x1, waiting for transfers between devices, body(): lax.all_to_all(model.reshape(64, 32, 256), 'bl', split_axis=0, concat_axi...  21.2 us
    all_to_all x1, starting transfers between devices, body(): lax.all_to_all(payload, 'bl', split_axis=0, concat_axis=0, tiled=True)  13.1 us
    all_to_all x1, starting transfers between devices, body(): lax.all_to_all(model.reshape(64, 32, 256), 'bl', split_axis=0, concat_axi...  11.5 us
    ppermute x1, waiting for transfers between devices, body(): lax.ppermute((chain_a.astype(F32) + next_a.astype(F32)).astype(BF16), 'ch...  11.2 us
    pallas_call x2, Pallas kernels, degrid(): pl.pallas_call(degrid_kernel(groups), out_shape=[jax.ShapeDtypeStruct((HA...  8.98 us
    ppermute x1, waiting for transfers between devices, body(): direct_a = lax.ppermute(prev_a, 'ch', down)  6.58 us
  transfers between devices with their start and end apart: 16, of which 12 were waited for; matrix products, arithmetic and copies ran while one was open for 2% of the time, Pallas kernels for 8%

profile of v1, /device:TPU:1, one launch (start us, length us, event | category | flops | bytes accessed | tf_op | source)
XLA Modules:
  0.0 219.4 jit_solution(15979207200518717415)
XLA Ops:
  0.0 3.6 %degrid1.1 = (bf16[1024,256]{1,0:T(8,128)(2,1)}, bf16[1024,256]{1,0:T(8,128)(2,1)}) custom-call(s32[1]{0:T(128)} %bitcast.where_ref, s32[4]{0:T(128)} %tile_ref.3, bf16[2048,256]{1,0:T(8,128)(2,1)} %kern_ref.3, bf16[4,64,16,256]{3,2,1,0:T(8,128)(2,1)} %facet_ref.3), custom_call_target="tpu_custom_call" | custom-call | tf_op jit(solution)/shard_map/degrid1/pallas_call | solution.py:59
  3.6 2.0 collective-permute-start
  5.6 1.3 collective-permute-start.2
  6.9 0.7 reshape.76.obs_ref
  7.6 2.0 payload.1
  9.6 13.1 %all-to-all-start.1 = ((bf16[64,32,128]{2,1,0:T(8,128)(2,1)}), bf16[64,32,128]{2,1,0:T(8,128)(2,1)S(1)}, u32[]{:S(2)}, u32[]{:S(2)}) async-start(bf16[64,32,128]{2,1,0:T(8,128)(2,1)} %bitcast.24), calls=%async_computation.1 | async-start | bytes 1048576 | tf_op jit(solution)/shard_map/all_to_all | solution.py:259
  22.7 5.4 %degrid3.1 = (bf16[1024,256]{1,0:T(8,128)(2,1)}, bf16[1024,256]{1,0:T(8,128)(2,1)}, bf16[1024,256]{1,0:T(8,128)(2,1)}, bf16[1024,256]{1,0:T(8,128)(2,1)}, bf16[1...) custom-call(s32[1]{0:T(128)} %bitcast.where_ref, s32[4]{0:T(128)} %tile_ref.3, bf16[2048,256]{1,0:T(8,128)(2,1)} %kern_ref.3, ...), custom_call_target="tpu_custom_call" | custom-call | tf_op jit(solution)/shard_map/degrid3/pallas_call | solution.py:59
  28.0 1.3 collective-permute-start.4
  29.5 1.2 add_convert_fusion.1
  30.8 1.2 add_convert_fusion
  32.0 2.7 %collective-permute-start.3 = (bf16[1024,256]{1,0:T(8,128)(2,1)S(1)}, bf16[1024,256]{1,0:T(8,128)(2,1)S(1)}, u32[]{:S(2)}, u32[]{:S(2)}) collective-permute-start(bf16[1024,256]{1,0:T(8,128)(2,1)S(1)} %add_convert_fusion), channel_id=1, source_target_pairs={{0,3},{1,0},{2,1},{3,2},{4,7},{5,4},{6,5},{7,6},{8,11},{9,8},{10,9... | collective-permute-start | bytes 1572872 | tf_op jit(solution)/shard_map/ppermute | solution.py:256
  34.7 6.6 %collective-permute-done.4.near_a = bf16[1024,256]{1,0:T(8,128)(2,1)S(1)} collective-permute-done((bf16[1024,256]{1,0:T(8,128)(2,1)}, bf16[1024,256]{1,0:T(8,128)(2,1)S(1)}, u32[]{:S(2)}, u32[]{:S(2)}) %collective-permute-start.4) | collective-permute-done | bytes 524320 | tf_op jit(solution)/shard_map/ppermute | solution.py:253
  41.3 2.2 %collective-permute-done.5.near_b = bf16[1024,256]{1,0:T(8,128)(2,1)S(1)} collective-permute-done((bf16[1024,256]{1,0:T(8,128)(2,1)}, bf16[1024,256]{1,0:T(8,128)(2,1)S(1)}, u32[]{:S(2)}, u32[]{:S(2)}) %collective-permute-start.5) | collective-permute-done | bytes 524320 | tf_op jit(solution)/shard_map/ppermute | solution.py:254
  43.5 11.2 %collective-permute-done.1.chain_a = bf16[1024,256]{1,0:T(8,128)(2,1)S(1)} collective-permute-done((bf16[1024,256]{1,0:T(8,128)(2,1)S(1)}, bf16[1024,256]{1,0:T(8,128)(2,1)S(1)}, u32[]{:S(2)}, u32[]{:S(2)}) %collective-permute-start.1) | collective-permute-done | bytes 524320 | tf_op jit(solution)/shard_map/ppermute | solution.py:255
  54.7 0.8 copy-done.4
  55.7 3.2 %add.21 = bf16[2048,256]{1,0:T(8,128)(2,1)} custom-call(bf16[1024,256]{1,0:T(8,128)(2,1)} %get-tuple-element.25.own_a, bf16[1024,256]{1,0:T(8,128)(2,1)} %get-tuple-element.26.own_b, bf16[1024,256]{1,0:T(8,128)(2,1)} %copy-done.4, bf16[1024,256]{1,0:T(8,128)(2,1)} %copy-done.5, bf16[1024,256]{1,0:T(8,128)(2,1)} %copy-done.2, bf16[1024,256]{1,0:T(8,128)(2,1)} %copy-done.3), custom_call_target="tpu_custom_call" | custom-call | tf_op jit(solution)/shard_map/add/pallas_call | solution.py:265
  58.9 11.5 %all-to-all-start = ((bf16[64,32,256]{2,1,0:T(8,128)(2,1)}), bf16[64,32,256]{2,1,0:T(8,128)(2,1)S(1)}, u32[]{:S(2)}, u32[]{:S(2)}) async-start(bf16[64,32,256]{2,1,0:T(8,128)(2,1)} %bitcast.22), calls=%async_computation | async-start | bytes 2097152 | tf_op jit(solution)/shard_map/all_to_all | solution.py:268
  71.1 0.7 fusion.own_ref
  71.8 6.0 %setup.1 = (bf16[2048,512]{1,0:T(8,128)(2,1)}, bf16[2048,128]{1,0:T(8,128)(2,1)}, bf16[16,2048]{1,0:T(8,128)(2,1)}, f32[2048,128]{1,0:T(8,128)}, f32[2048,128]{1,0:T(8,128)}, /*index=5*/f32[2048,128]{1,0:T(8,128)}) custom-call(bf16[2048,128]{1,0:T(8,128)(2,1)} %bitcast.23, f32[1,512]{1,0:T(1,128)} %bitcast.29, f32[1,128]{1,0:T(1,128)} %fusion.own_ref), custom_call_target="tpu_custom_call" | custom-call | tf_op jit(solution)/shard_map/setup/pallas_call | solution.py:130
  77.8 21.2 %all-to-all-done = bf16[64,32,256]{2,1,0:T(8,128)(2,1)S(1)} async-done(((bf16[64,32,256]{2,1,0:T(8,128)(2,1)}), bf16[64,32,256]{2,1,0:T(8,128)(2,1)S(1)}, u32[]{:S(2)}, u32[]{:S(2)}) %all-to-all-start) | async-done | bytes 1048608 | tf_op jit(solution)/shard_map/all_to_all | solution.py:268
  99.0 1.0 copy-done
  100.0 6.3 %iterate0.1.mid_ref = f32[8,256]{1,0:T(8,128)} custom-call(bf16[2048,256]{1,0:T(8,128)(2,1)} %bitcast.18, bf16[16,2048]{1,0:T(8,128)(2,1)} %get-tuple-element.33.refs_1_, f32[2048,128]{1,0:T(8,128)} %get-tuple-element.34.refs_2_, f32[2048,128]{1,0:T(8,128)} %get-tuple-element.35.refs_3_, f32[2048,128]{1,0:T(8,128)} %get-tuple-element.36.refs_4_), custom_call_target="tpu_custom_call" | custom-call | tf_op jit(solution)/shard_map/iterate0/pallas_call | solution.py:198
  106.3 1.5 collective-permute-start.6
  107.7 1.2 collective-permute-done.7.high_ref
  109.0 1.2 collective-permute-done.6.low_ref
  110.8 1.5 smooth.4
  112.3 19.5 %all_to_all.25 = bf16[64,8,256]{2,1,0:T(8,128)(2,1)} all-to-all(bf16[64,8,256]{2,1,0:T(8,128)(2,1)} %get-tuple-element.39), channel_id=1, replica_groups=mesh['bl'=64,'ch'=4] {'bl'}, dimensions={0} | all-to-all | bytes 524288 | tf_op jit(solution)/shard_map/all_to_all | solution.py:280
  131.8 9.4 %iterate.3.mid_ref = f32[8,256]{1,0:T(8,128)} custom-call(bf16[2048,256]{1,0:T(8,128)(2,1)} %bitcast.19, bf16[16,2048]{1,0:T(8,128)(2,1)} %get-tuple-element.33.refs_1_, f32[2048,128]{1,0:T(8,128)} %get-tuple-element.34.refs_2_, f32[2048,128]{1,0:T(8,128)} %get-tuple-element.35.refs_3_, f32[2048,128]{1,0:T(8,128)} %get-tuple-element.36.refs_4_, ...), custom_call_target="tpu_custom_call" | custom-call | tf_op jit(solution)/shard_map/iterate/pallas_call | solution.py:198
  141.5 1.2 collective-permute-start.8
  142.6 1.2 collective-permute-done.9.high_ref
  143.9 1.5 collective-permute-done.8.low_ref
  145.4 0.6 copy-done.11
  146.0 1.5 smooth.5
  147.5 19.5 %all_to_all.26 = bf16[64,8,256]{2,1,0:T(8,128)(2,1)} all-to-all(bf16[64,8,256]{2,1,0:T(8,128)(2,1)} %get-tuple-element.41), channel_id=1, replica_groups=mesh['bl'=64,'ch'=4] {'bl'}, dimensions={0} | all-to-all | bytes 524288 | tf_op jit(solution)/shard_map/all_to_all | solution.py:280
  167.0 9.4 %iterate.4.mid_ref = f32[8,256]{1,0:T(8,128)} custom-call(bf16[2048,256]{1,0:T(8,128)(2,1)} %bitcast.20, bf16[16,2048]{1,0:T(8,128)(2,1)} %get-tuple-element.33.refs_1_, f32[2048,128]{1,0:T(8,128)} %get-tuple-element.34.refs_2_, f32[2048,128]{1,0:T(8,128)} %get-tuple-element.35.refs_3_, f32[2048,128]{1,0:T(8,128)} %get-tuple-element.36.refs_4_, ...), custom_call_target="tpu_custom_call" | custom-call | tf_op jit(solution)/shard_map/iterate/pallas_call | solution.py:198
  176.7 1.2 collective-permute-start.10
  177.9 1.2 collective-permute-done.11.high_ref
  179.1 1.5 collective-permute-done.10.low_ref
  181.2 1.5 smooth.6
  182.8 19.5 %all_to_all.27 = bf16[64,8,256]{2,1,0:T(8,128)(2,1)} all-to-all(bf16[64,8,256]{2,1,0:T(8,128)(2,1)} %get-tuple-element.43), channel_id=1, replica_groups=mesh['bl'=64,'ch'=4] {'bl'}, dimensions={0} | all-to-all | bytes 524288 | tf_op jit(solution)/shard_map/all_to_all | solution.py:280
  202.3 9.4 %iterate.5.mid_ref = f32[8,256]{1,0:T(8,128)} custom-call(bf16[2048,256]{1,0:T(8,128)(2,1)} %bitcast.21, bf16[16,2048]{1,0:T(8,128)(2,1)} %get-tuple-element.33.refs_1_, f32[2048,128]{1,0:T(8,128)} %get-tuple-element.34.refs_2_, f32[2048,128]{1,0:T(8,128)} %get-tuple-element.35.refs_3_, f32[2048,128]{1,0:T(8,128)} %get-tuple-element.36.refs_4_, ...), custom_call_target="tpu_custom_call" | custom-call | tf_op jit(solution)/shard_map/iterate/pallas_call | solution.py:198
  212.0 1.2 collective-permute-start.12
  213.1 1.2 collective-permute-done.13.high_ref
  214.4 1.5 collective-permute-done.12.low_ref
  215.9 0.6 copy-done.14
  216.5 1.4 smooth.7
  217.9 0.8 reshape.83
  218.7 0.7 copy.10
  (42 shorter events, 3.3 us)
Async XLA Ops:
  0.0 6.9 %copy-start.6 = (bf16[16,2,2048]{2,1,0:T(2,128)(2,1)S(1)}, bf16[16,2,2048]{2,1,0:T(2,128)(2,1)}, u32[]{:S(2)}) copy-start(bf16[16,2,2048]{2,1,0:T(2,128)(2,1)} %param.10) | copy-start | bytes 393220
  3.6 25.9 %collective-permute-start = (bf16[1024,256]{1,0:T(8,128)(2,1)}, bf16[1024,256]{1,0:T(8,128)(2,1)S(1)}, u32[]{:S(2)}, u32[]{:S(2)}) collective-permute-start(bf16[1024,256]{1,0:T(8,128)(2,1)} %get-tuple-element.27), channel_id=1, source_target_pairs={{0,1},{1,2},{2,3},{3,0},{4,5},{5,6},{6,7},{7,4},{8,9},{9,10},{10,1... | collective-permute-start | bytes 1572872 | tf_op jit(solution)/shard_map/ppermute | solution.py:250
  5.6 25.1 %collective-permute-start.2 = (bf16[1024,256]{1,0:T(8,128)(2,1)}, bf16[1024,256]{1,0:T(8,128)(2,1)S(1)}, u32[]{:S(2)}, u32[]{:S(2)}) collective-permute-start(bf16[1024,256]{1,0:T(8,128)(2,1)} %get-tuple-element.29), channel_id=1, source_target_pairs={{0,3},{1,0},{2,1},{3,2},{4,7},{5,4},{6,5},{7,6},{8,11},{9,8},{10,9... | collective-permute-start | bytes 1572872 | tf_op jit(solution)/shard_map/ppermute | solution.py:251
  9.6 49.3 %all-to-all-start.1 = ((bf16[64,32,128]{2,1,0:T(8,128)(2,1)}), bf16[64,32,128]{2,1,0:T(8,128)(2,1)S(1)}, u32[]{:S(2)}, u32[]{:S(2)}) async-start(bf16[64,32,128]{2,1,0:T(8,128)(2,1)} %bitcast.24), calls=%async_computation.1 | async-start | bytes 1048576 | tf_op jit(solution)/shard_map/all_to_all | solution.py:259
  28.0 13.2 %collective-permute-start.4 = (bf16[1024,256]{1,0:T(8,128)(2,1)}, bf16[1024,256]{1,0:T(8,128)(2,1)S(1)}, u32[]{:S(2)}, u32[]{:S(2)}) collective-permute-start(bf16[1024,256]{1,0:T(8,128)(2,1)} %get-tuple-element.31), channel_id=1, source_target_pairs={{0,3},{1,0},{2,1},{3,2},{4,7},{5,4},{6,5},{7,6},{8,11},{9,8},{10,9... | collective-permute-start | bytes 1572872 | tf_op jit(solution)/shard_map/ppermute | solution.py:253
  29.3 14.2 %collective-permute-start.5 = (bf16[1024,256]{1,0:T(8,128)(2,1)}, bf16[1024,256]{1,0:T(8,128)(2,1)S(1)}, u32[]{:S(2)}, u32[]{:S(2)}) collective-permute-start(bf16[1024,256]{1,0:T(8,128)(2,1)} %get-tuple-element.32), channel_id=1, source_target_pairs={{0,1},{1,2},{2,3},{3,0},{4,5},{5,6},{6,7},{7,4},{8,9},{9,10},{10,1... | collective-permute-start | bytes 1572872 | tf_op jit(solution)/shard_map/ppermute | solution.py:254
  30.7 24.0 %collective-permute-start.1 = (bf16[1024,256]{1,0:T(8,128)(2,1)S(1)}, bf16[1024,256]{1,0:T(8,128)(2,1)S(1)}, u32[]{:S(2)}, u32[]{:S(2)}) collective-permute-start(bf16[1024,256]{1,0:T(8,128)(2,1)S(1)} %add_convert_fusion.1), channel_id=1, source_target_pairs={{0,1},{1,2},{2,3},{3,0},{4,5},{5,6},{6,7},{7,4},{8,9},{9,10},{10,1... | collective-permute-start | bytes 1572872 | tf_op jit(solution)/shard_map/ppermute | solution.py:255
  32.0 22.8 %collective-permute-start.3 = (bf16[1024,256]{1,0:T(8,128)(2,1)S(1)}, bf16[1024,256]{1,0:T(8,128)(2,1)S(1)}, u32[]{:S(2)}, u32[]{:S(2)}) collective-permute-start(bf16[1024,256]{1,0:T(8,128)(2,1)S(1)} %add_convert_fusion), channel_id=1, source_target_pairs={{0,3},{1,0},{2,1},{3,2},{4,7},{5,4},{6,5},{7,6},{8,11},{9,8},{10,9... | collective-permute-start | bytes 1572872 | tf_op jit(solution)/shard_map/ppermute | solution.py:256
  41.3 13.4 %copy-start.2 = (bf16[1024,256]{1,0:T(8,128)(2,1)}, bf16[1024,256]{1,0:T(8,128)(2,1)S(1)}, u32[]{:S(2)}) copy-start(bf16[1024,256]{1,0:T(8,128)(2,1)S(1)} %collective-permute-done.4.near_a) | copy-start | bytes 1572868
  43.5 11.3 %copy-start.3 = (bf16[1024,256]{1,0:T(8,128)(2,1)}, bf16[1024,256]{1,0:T(8,128)(2,1)S(1)}, u32[]{:S(2)}) copy-start(bf16[1024,256]{1,0:T(8,128)(2,1)S(1)} %collective-permute-done.5.near_b) | copy-start | bytes 1572868
  54.7 0.8 copy-start.4
  54.7 1.0 copy-start.5
  58.9 11.6 %copy-start.15 = (s32[512]{0:T(512)S(1)}, s32[512]{0:T(512)}, u32[]{:S(2)}) copy-start(s32[512]{0:T(512)} %param.13) | copy-start | bytes 6148
  58.9 12.9 %copy-start.1 = (bf16[64,32,128]{2,1,0:T(8,128)(2,1)}, bf16[64,32,128]{2,1,0:T(8,128)(2,1)S(1)}, u32[]{:S(2)}) copy-start(bf16[64,32,128]{2,1,0:T(8,128)(2,1)S(1)} %all-to-all-done.1) | copy-start | bytes 1572868
  58.9 40.1 %all-to-all-start = ((bf16[64,32,256]{2,1,0:T(8,128)(2,1)}), bf16[64,32,256]{2,1,0:T(8,128)(2,1)S(1)}, u32[]{:S(2)}, u32[]{:S(2)}) async-start(bf16[64,32,256]{2,1,0:T(8,128)(2,1)} %bitcast.22), calls=%async_computation | async-start | bytes 2097152 | tf_op jit(solution)/shard_map/all_to_all | solution.py:268
  99.0 1.0 copy-start
  106.3 2.7 %collective-permute-start.7 = (f32[8,256]{1,0:T(8,128)}, f32[8,256]{1,0:T(8,128)S(1)}, u32[]{:S(2)}, u32[]{:S(2)}) collective-permute-start(f32[8,256]{1,0:T(8,128)} %iterate0.1.mid_ref), channel_id=1, source_target_pairs={{0,3},{1,0},{2,1},{3,2},{4,7},{5,4},{6,5},{7,6},{8,11},{9,8},{10,9... | collective-permute-start | bytes 24584 | tf_op jit(solution)/shard_map/ppermute | solution.py:277
  106.3 3.9 %collective-permute-start.6 = (f32[8,256]{1,0:T(8,128)}, f32[8,256]{1,0:T(8,128)S(1)}, u32[]{:S(2)}, u32[]{:S(2)}) collective-permute-start(f32[8,256]{1,0:T(8,128)} %iterate0.1.mid_ref), channel_id=1, source_target_pairs={{0,1},{1,2},{2,3},{3,0},{4,5},{5,6},{6,7},{7,4},{8,9},{9,10},{10,1... | collective-permute-start | bytes 24584 | tf_op jit(solution)/shard_map/ppermute | solution.py:276
  109.0 1.2 copy-start.7
  110.2 0.6 copy-start.10
  141.2 2.7 %collective-permute-start.9 = (f32[8,256]{1,0:T(8,128)}, f32[8,256]{1,0:T(8,128)S(1)}, u32[]{:S(2)}, u32[]{:S(2)}) collective-permute-start(f32[8,256]{1,0:T(8,128)} %iterate.3.mid_ref), channel_id=1, source_target_pairs={{0,3},{1,0},{2,1},{3,2},{4,7},{5,4},{6,5},{7,6},{8,11},{9,8},{10,9... | collective-permute-start | bytes 24584 | tf_op jit(solution)/shard_map/ppermute | solution.py:277
  141.5 3.9 %collective-permute-start.8 = (f32[8,256]{1,0:T(8,128)}, f32[8,256]{1,0:T(8,128)S(1)}, u32[]{:S(2)}, u32[]{:S(2)}) collective-permute-start(f32[8,256]{1,0:T(8,128)} %iterate.3.mid_ref), channel_id=1, source_target_pairs={{0,1},{1,2},{2,3},{3,0},{4,5},{5,6},{6,7},{7,4},{8,9},{9,10},{10,1... | collective-permute-start | bytes 24584 | tf_op jit(solution)/shard_map/ppermute | solution.py:276
  143.9 1.5 copy-start.8
  145.4 0.6 copy-start.11
  176.4 2.7 %collective-permute-start.11 = (f32[8,256]{1,0:T(8,128)}, f32[8,256]{1,0:T(8,128)S(1)}, u32[]{:S(2)}, u32[]{:S(2)}) collective-permute-start(f32[8,256]{1,0:T(8,128)} %iterate.4.mid_ref), channel_id=1, source_target_pairs={{0,3},{1,0},{2,1},{3,2},{4,7},{5,4},{6,5},{7,6},{8,11},{9,8},{10,9... | collective-permute-start | bytes 24584 | tf_op jit(solution)/shard_map/ppermute | solution.py:277
  176.7 3.9 %collective-permute-start.10 = (f32[8,256]{1,0:T(8,128)}, f32[8,256]{1,0:T(8,128)S(1)}, u32[]{:S(2)}, u32[]{:S(2)}) collective-permute-start(f32[8,256]{1,0:T(8,128)} %iterate.4.mid_ref), channel_id=1, source_target_pairs={{0,1},{1,2},{2,3},{3,0},{4,5},{5,6},{6,7},{7,4},{8,9},{9,10},{10,1... | collective-permute-start | bytes 24584 | tf_op jit(solution)/shard_map/ppermute | solution.py:276
  179.1 1.5 copy-start.9
  180.6 0.6 copy-start.12
  211.7 2.7 %collective-permute-start.13 = (f32[8,256]{1,0:T(8,128)}, f32[8,256]{1,0:T(8,128)S(1)}, u32[]{:S(2)}, u32[]{:S(2)}) collective-permute-start(f32[8,256]{1,0:T(8,128)} %iterate.5.mid_ref), channel_id=1, source_target_pairs={{0,3},{1,0},{2,1},{3,2},{4,7},{5,4},{6,5},{7,6},{8,11},{9,8},{10,9... | collective-permute-start | bytes 24584 | tf_op jit(solution)/shard_map/ppermute | solution.py:277
  212.0 3.9 %collective-permute-start.12 = (f32[8,256]{1,0:T(8,128)}, f32[8,256]{1,0:T(8,128)S(1)}, u32[]{:S(2)}, u32[]{:S(2)}) collective-permute-start(f32[8,256]{1,0:T(8,128)} %iterate.5.mid_ref), channel_id=1, source_target_pairs={{0,1},{1,2},{2,3},{3,0},{4,5},{5,6},{6,7},{7,4},{8,9},{9,10},{10,1... | collective-permute-start | bytes 24584 | tf_op jit(solution)/shard_map/ppermute | solution.py:276
  214.4 1.5 copy-start.13
  215.9 0.6 copy-start.14

commit v2 on v1

v2 whole, which is shorter than its diff:
```python
import jax
import jax.numpy as jnp
from jax import lax
from jax.experimental import pallas as pl
from jax.experimental.pallas import tpu as pltpu
from jax.sharding import Mesh, PartitionSpec as P

S = 512
ND = 8
ITERS = 4
LANES = 128
ROWS = 2048
HALF = 512
CHUNK = 256
F32 = jnp.float32
BF16 = jnp.bfloat16
BL = ("y", "z", "core")
SMALL = pltpu.CompilerParams(vmem_limit_bytes=16 << 20)


def nt(a, b):
    return lax.dot_general(a, b, (((1,), (1,)), ((), ())), preferred_element_type=F32)


def nn(a, b):
    return lax.dot_general(a, b, (((1,), (0,)), ((), ())), preferred_element_type=F32)


def iota(shape, dim):
    return lax.broadcasted_iota(jnp.int32, shape, dim)


def lane_order():
    lane = iota((256, 256), 0)
    source = (lane & 15) * 16 + ((lane >> 4) & 7) * 2 + (lane >> 7)
    return (iota((256, 256), 1) == source).astype(F32).astype(BF16)


def in_hbm(x):
    return pltpu.with_memory_space_constraint(x, pltpu.HBM)


def full(shape):
    return pl.BlockSpec(shape, lambda i, *scalars: (0,) * len(shape))


def degrid_kernel(count):
    def run(where_ref, tile_ref, kern_ref, *refs):
        facets, outs, tables = refs[:count], refs[count : 3 * count], refs[3 * count : 4 * count]
        order = lane_order()
        for index in range(count):
            for tile in range(4):
                tables[index][tile] = nn(order, facets[index][tile].reshape(256, 256)).astype(BF16)
        for block in range(4):
            rows = kern_ref[block * 16 : (block + 1) * 16].reshape(256, 256)
            place = slice((block % 2) * 256, (block % 2) * 256 + 256)
            for index in range(count):
                outs[2 * index + block // 2][place, :] = nt(rows, tables[index][tile_ref[block]]).astype(BF16)

    return run


def degrid(where, tile_of, kernel, facet_grid, groups):
    count = len(groups)

    def facet_spec(shift):
        return pl.BlockSpec((4, 16, 16, 256), lambda i, where, tile: (0, (where[0] + shift) & 3, 0, 0))

    half = jax.ShapeDtypeStruct((HALF, 256), BF16)
    table = pltpu.HBM((4, 256, 256), BF16)
    return pl.pallas_call(
        degrid_kernel(count),
        out_shape=[half] * (2 * count) + [table] * count,
        grid_spec=pltpu.PrefetchScalarGridSpec(
            num_scalar_prefetch=2,
            grid=(1,),
            in_specs=[full((64, 16, 256))] + [facet_spec(g) for g in groups],
            out_specs=[full((HALF, 256))] * (2 * count) + [full((4, 256, 256))] * count,
        ),
        compiler_params=SMALL,
    )(where, tile_of, in_hbm(kernel), *([in_hbm(facet_grid)] * count))


def late_kernel(jobs):
    def run(pay_ref, *refs):
        tables, outs = refs[:3], refs[3:]
        weight = (iota((LANES, 256), 0) == 52).astype(F32).astype(BF16)
        for half in range(2):

            def step(block, carry, half=half):
                segments = pl.ds(half * 32 + block * 16, 16)
                rows = pay_ref[segments, :16, :].reshape(256, 256)
                small = pay_ref[segments, 16:24, 128:].astype(F32).reshape(128, LANES)
                early = nn(small.astype(BF16), weight).reshape(16, 8, 256)
                late = nn(pltpu.roll(small, 64, 1).astype(BF16), weight).reshape(16, 8, 256)
                tile = jnp.concatenate([early, late], axis=1).reshape(256, 256)
                masked = [rows * (tile == float(t)).astype(F32).astype(BF16) for t in range(4)]
                place = pl.ds(pl.multiple_of(block * 256, 256), 256)
                for index, out in jobs[half]:
                    total = nt(masked[0], tables[index][0])
                    for t in range(1, 4):
                        total = total + nt(masked[t], tables[index][t])
                    outs[out][place, :] = total.astype(BF16)
                return carry

            lax.fori_loop(0, 2, step, 0, unroll=2)

    return run


def late_degrid(payload, tables, jobs, last):
    return pl.pallas_call(
        late_kernel(jobs),
        out_shape=[jax.ShapeDtypeStruct((HALF, 256), BF16)] * 2 + [last] * 2,
        compiler_params=SMALL,
        name="late",
    )(payload, *[in_hbm(table) for table in tables])


def payload_kernel(tile_ref, obs_ref, flag_ref, pair_ref, kern_ref, out_ref, kept_ref, stacked_ref):
    out_ref[:, :16, :] = kern_ref[...]
    kept = (1 - flag_ref[...]).astype(F32)
    pair = pair_ref[...]
    high = (pair >> 3).astype(F32)
    low = (pair & 7).astype(F32)
    block = iota((1, ROWS), 1) >> 9
    tile = jnp.where(block < 2, jnp.where(block == 0, tile_ref[0], tile_ref[1]), jnp.where(block == 2, tile_ref[2], tile_ref[3]))
    fill = jnp.zeros((LANES - 53, ROWS), F32)
    obs = obs_ref[...].astype(F32)
    stacked_ref[...] = jnp.concatenate([obs[:, 0], obs[:, 1], kept, high, low, tile.astype(F32), fill], axis=0)
    source = iota((LANES, 256), 0)
    col = iota((LANES, 256), 1)
    pick = (source == 32 + (col & 15)) & ((col < 32) | (col >= 128))
    pick = pick.astype(F32).astype(BF16)
    rest = (iota((LANES, LANES), 1) >= 32).astype(F32)

    def step(part, carry):
        turned = stacked_ref[:, pl.ds(pl.multiple_of(part * 128, 128), 128)].T
        wide = nn(turned.astype(BF16), pick)
        value = turned * (wide[:, :128] + rest)
        moved = pltpu.roll(value, 64, 1).reshape(4, 4, 8, LANES)
        value = value.reshape(4, 4, 8, LANES)
        segments = pl.ds(part * 4, 4)
        out_ref[segments, 16:24, :128] = (value[:, 0] + moved[:, 1]).astype(BF16)
        out_ref[segments, 16:24, 128:] = (value[:, 2] + moved[:, 3]).astype(BF16)
        kept = wide[:, 128:].reshape(4, 32, LANES)[:, :16].reshape(64, LANES).astype(BF16)
        kept_ref[pl.ds(pl.multiple_of(part * 64, 64), 64), :] = kept
        return carry

    lax.fori_loop(0, ROWS // 128, step, 0, unroll=4)


def make_payload(tile_of, observed, flags, pairs, kernel):
    return pl.pallas_call(
        payload_kernel,
        out_shape=[jax.ShapeDtypeStruct((64, 24, 256), BF16), jax.ShapeDtypeStruct((1024, LANES), BF16)],
        grid_spec=pltpu.PrefetchScalarGridSpec(
            num_scalar_prefetch=1,
            grid=(1,),
            in_specs=[
                full((16, 2, ROWS)),
                full((16, ROWS)),
                full((2, ROWS)),
                pl.BlockSpec((64, 16, 256), lambda i, tile: (0, 1, 0)),
            ],
            out_specs=[full((64, 24, 256)), full((1024, LANES))],
            scratch_shapes=[pltpu.VMEM((LANES, ROWS), F32)],
        ),
        compiler_params=SMALL,
        name="payload",
    )(tile_of, in_hbm(observed), in_hbm(flags), in_hbm(pairs), in_hbm(kernel))


def setup_kernel(pay_ref, order_ref, own_ref, ohq_ref, ohp_ref, opt_ref, vre_ref, vim_ref, kept_ref):
    source = iota((LANES, 5 * LANES), 0)
    col = iota((LANES, 5 * LANES), 1)
    piece = col >> 7
    weight = ((source == 16 * piece + (col & 15)) & (piece < 2)).astype(F32)
    weight = weight + 8.0 * ((source == 49) & (piece == 2)).astype(F32) + ((source == 51) & (piece == 2)).astype(F32)
    weight = weight + 8.0 * ((source == 48) & (piece == 3)).astype(F32) + ((source == 50) & (piece == 3)).astype(F32)
    weight = weight + ((source == 32 + (col & 15)) & (piece == 4)).astype(F32)
    weight = weight.astype(BF16)
    order = order_ref[...]
    own = own_ref[...]

    def step(i, carry):
        value = pay_ref[pl.ds(pl.multiple_of(i * 8, 8), 8), 16:24, :].astype(F32).reshape(64, 256)
        left, right = value[:, :128], value[:, 128:]
        value = jnp.concatenate([left, pltpu.roll(left, 64, 1), right, pltpu.roll(right, 64, 1)], axis=0)
        wide = nn(value.astype(BF16), weight).reshape(4, 8, 8, 5 * LANES)
        for part in range(2):
            rows = pl.ds(pl.multiple_of(i * 128 + part * 1024, 128), 128)
            mine = jnp.concatenate([wide[2 * part], wide[2 * part + 1]], axis=1).reshape(128, 5 * LANES)
            vre_ref[rows, :] = mine[:, :128].astype(BF16)
            vim_ref[rows, :] = mine[:, 128:256].astype(BF16)
            second = mine[:, 256:384]
            for quarter in range(4):
                lanes = slice(quarter * 128, (quarter + 1) * 128)
                ohq_ref[rows, lanes] = (second == order[:, lanes]).astype(F32).astype(BF16)
            near = (mine[:, 384:512] == own).astype(F32)
            ohp_ref[rows, :] = near.astype(BF16)
            opt_ref[:, rows] = near.T[:16, :].astype(BF16)
            if part == 1:
                kept_ref[pl.ds(pl.multiple_of(i * 128, 128), 128), :] = mine[:, 512:].astype(BF16)
        return carry

    lax.fori_loop(0, 8, step, 0)


def make_setup(payload, order, own):
    shapes = [
        jax.ShapeDtypeStruct((ROWS, S), BF16),
        jax.ShapeDtypeStruct((ROWS, LANES), BF16),
        jax.ShapeDtypeStruct((16, ROWS), BF16),
        pltpu.HBM((ROWS, LANES), BF16),
        pltpu.HBM((ROWS, LANES), BF16),
        pltpu.HBM((1024, LANES), BF16),
    ]
    return pl.pallas_call(setup_kernel, out_shape=shapes, compiler_params=SMALL, name="setup")(payload, order, own)


def over_directions(x):
    x = x + pltpu.roll(x, 16, 1)
    x = x + pltpu.roll(x, 32, 1)
    return x + pltpu.roll(x, 64, 1)


def iterate_kernel(first):
    def run(*refs):
        if first:
            model_a, *parts, opt_ref, vre_ref, vim_ref, out_ref, model_b, terms_ref = refs
            add_kernel(*parts, model_b)
        else:
            model_a, model_b, opt_ref, vre_ref, vim_ref, ohq_ref, ohp_ref, all_ref, own_ref, out_ref, terms_ref = refs
            all_gains = all_ref[...]
            own = own_ref[...]
            high = own.astype(BF16).astype(F32)
            near_gains = jnp.concatenate([high, own - high, jnp.zeros((LANES - 16, 256), F32)], axis=0).astype(BF16)

        for i in range(ROWS // CHUNK):
            rows = slice(i * CHUNK, (i + 1) * CHUNK)
            model = (model_a if i < 4 else model_b)[(i % 4) * CHUNK : (i % 4 + 1) * CHUNK, :].astype(F32)
            model_re, model_im = model[:, :128], model[:, 128:]
            if first:
                prod_re = pred_re = model_re
                prod_im = pred_im = model_im
            else:
                far = nn(ohq_ref[rows, :], all_gains)
                near = nn(ohp_ref[rows, :], near_gains)
                far_re, far_im = far[:, :128], far[:, 128:]
                near_re, near_im = near[:, :128], near[:, 128:]
                prod_re = model_re * far_re + model_im * far_im
                prod_im = model_im * far_re - model_re * far_im
                pred_re = near_re * prod_re - near_im * prod_im
                pred_im = near_re * prod_im + near_im * prod_re
            res_re = vre_ref[rows, :].astype(F32) - over_directions(pred_re)
            res_im = vim_ref[rows, :].astype(F32) - over_directions(pred_im)
            terms = jnp.concatenate(
                [
                    prod_re * res_re + prod_im * res_im,
                    prod_re * res_im - prod_im * res_re,
                    prod_re * prod_re + prod_im * prod_im,
                ],
                axis=1,
            )
            top = terms.astype(BF16)
            terms_ref[rows, :384] = top
            terms_ref[rows, 384:] = (terms - top.astype(F32)).astype(BF16)

        acc = nn(opt_ref[...], terms_ref[...])[:8]
        acc = acc[:, :384] + acc[:, 384:]
        sum_re, sum_im, power = acc[:, :128], acc[:, 128:256], acc[:, 256:]
        if first:
            gain_re = jnp.ones((8, 128), F32)
            gain_im = jnp.zeros((8, 128), F32)
        else:
            gain_re, gain_im = own[:, :128], own[:, 128:]
        new_re = (sum_re + gain_re * power) / (power + 1.0)
        new_im = (sum_im + gain_im * power) / (power + 1.0)
        out_ref[:, :128] = (gain_re + new_re) * 0.5
        out_ref[:, 128:] = (gain_im + new_im) * 0.5

    return run


def iterate(args, first):
    return pl.pallas_call(
        iterate_kernel(first),
        out_shape=[jax.ShapeDtypeStruct((8, 256), F32)] + [jax.ShapeDtypeStruct((1024, 256), BF16)] * first,
        scratch_shapes=[pltpu.VMEM((ROWS, 768), BF16)],
        compiler_params=SMALL,
        name="iterate0" if first else "iterate",
    )(*args)


def smooth_kernel(spread):
    def run(where_ref, mid_ref, low_ref, high_ref, out_ref, *more):
        chan = iota((8, LANES), 1) & 15
        whole = chan + 16 * where_ref[0]
        has_left = (whole > 0).astype(F32)
        has_right = (whole < 63).astype(F32)
        for part in range(2):
            lanes = slice(part * 128, (part + 1) * 128)
            mid = mid_ref[:, lanes]
            left = jnp.where(chan == 0, pltpu.roll(low_ref[:, lanes], 113, 1), pltpu.roll(mid, 1, 1))
            right = jnp.where(chan == 15, pltpu.roll(high_ref[:, lanes], 15, 1), pltpu.roll(mid, 127, 1))
            total = 0.25 * has_left * left + 0.5 * mid + 0.25 * has_right * right
            out_ref[:, lanes] = total / (0.5 + 0.25 * has_left + 0.25 * has_right)
        if spread:
            more[0][...] = jnp.broadcast_to(out_ref[...].astype(BF16)[None], (32, 8, 256))

    return run


def smooth(where, mid, low, high, spread):
    shapes = [jax.ShapeDtypeStruct((8, 256), F32)]
    if spread:
        shapes.append(jax.ShapeDtypeStruct((32, 8, 256), BF16))
    smem = pl.BlockSpec(memory_space=pltpu.SMEM)
    vmem = pl.BlockSpec(memory_space=pltpu.VMEM)
    return pl.pallas_call(
        smooth_kernel(spread),
        out_shape=shapes,
        in_specs=[smem, vmem, vmem, vmem],
        out_specs=[vmem] * len(shapes),
        compiler_params=SMALL,
        name="smooth",
    )(where, mid, low, high)


def pair_kernel(left_ref, right_ref, out_ref):
    for part in range(2):
        rows = slice(part * 256, (part + 1) * 256)
        out_ref[rows, :] = (left_ref[rows, :].astype(F32) + right_ref[rows, :].astype(F32)).astype(BF16)


def pair_sum(left, right):
    return pl.pallas_call(
        pair_kernel, out_shape=jax.ShapeDtypeStruct((HALF, 256), BF16), compiler_params=SMALL, name="pair"
    )(left, right)


def add_kernel(own_a, own_b, chain_a, chain_b, near_a, near_b, kept_ref, out_ref):
    for half, parts in ((0, (own_a, chain_a, near_a)), (1, (own_b, chain_b, near_b))):
        for part in range(2):
            near = slice(part * 256, (part + 1) * 256)
            rows = slice(half * HALF + part * 256, half * HALF + (part + 1) * 256)
            total = parts[0][near, :].astype(F32) + parts[1][near, :].astype(F32) + parts[2][near, :].astype(F32)
            kept = kept_ref[rows, :].astype(F32)
            out_ref[rows, :128] = (total[:, :128] * kept).astype(BF16)
            out_ref[rows, 128:] = (total[:, 128:] * kept).astype(BF16)


def total(*parts):
    return pl.pallas_call(
        add_kernel, out_shape=jax.ShapeDtypeStruct((1024, 256), BF16), compiler_params=SMALL, name="add"
    )(*parts)


UP = [(i, (i + 1) % 4) for i in range(4)]
DOWN = [(i, (i + 3) % 4) for i in range(4)]


def last_legs(chain_a, chain_b, direct_a, direct_b, next_a, prev_b):
    chain_a = lax.ppermute(pair_sum(chain_a, next_a), "ch", UP)
    chain_b = lax.ppermute(pair_sum(chain_b, prev_b), "ch", DOWN)
    return chain_a, chain_b, direct_a, direct_b


def exchange(value):
    return lax.all_to_all(value, BL, split_axis=0, concat_axis=0, tiled=True)


def body(facet_grid, kernel, tile_of, observed, flags, pairs, solver_order):
    where = lax.axis_index("ch").astype(jnp.int32).reshape(1)
    kernel = kernel.reshape(64, 32, 256)
    payload, kept_a = make_payload(tile_of, observed, flags, pairs, kernel)
    arrived = exchange(payload)

    mine = lax.dynamic_slice(solver_order, (8 * lax.axis_index(BL),), (8,))
    own_row = jnp.concatenate([mine, mine, jnp.full((LANES - 16,), -1, jnp.int32)]).astype(F32).reshape(1, LANES)
    order_row = solver_order.reshape(32, 2, 8).transpose(1, 0, 2).astype(F32).reshape(1, S)

    far_a, far_b, table2 = degrid(where, tile_of, kernel, facet_grid, (2,))
    chain_a = lax.ppermute(far_a, "ch", UP)
    chain_b = lax.ppermute(far_b, "ch", DOWN)
    next_a, next_b, prev_a, prev_b, own_a, own_b, table1, table3, table0 = degrid(
        where, tile_of, kernel, facet_grid, (1, 3, 0)
    )
    direct_a = lax.ppermute(prev_a, "ch", DOWN)
    direct_b = lax.ppermute(next_b, "ch", UP)
    legs = last_legs(chain_a, chain_b, direct_a, direct_b, next_a, prev_b)
    model_a = total(own_a, own_b, *legs, kept_a)

    near = jax.ShapeDtypeStruct((HALF, 256), BF16)
    away = pltpu.HBM((HALF, 256), BF16)
    far_a, far_b, prev_a, next_b = late_degrid(
        arrived, (table2, table3, table1), (((0, 0), (1, 2)), ((0, 1), (2, 3))), near
    )
    chain_a = lax.ppermute(far_a, "ch", UP)
    chain_b = lax.ppermute(far_b, "ch", DOWN)
    direct_a = lax.ppermute(prev_a, "ch", DOWN)
    direct_b = lax.ppermute(next_b, "ch", UP)
    next_a, prev_b, own_a, own_b = late_degrid(
        arrived, (table1, table3, table0), (((0, 0), (2, 2)), ((1, 1), (2, 3))), away
    )
    ohq, ohp, opt, vis_re, vis_im, kept_b = make_setup(arrived, order_row, own_row)
    legs = last_legs(chain_a, chain_b, direct_a, direct_b, next_a, prev_b)
    model_a = exchange(model_a.reshape(64, 16, 256)).reshape(1024, 256)

    for step in range(ITERS):
        if step == 0:
            parts = (in_hbm(own_a), in_hbm(own_b), *legs, in_hbm(kept_b))
            mid, model_b = iterate((model_a, *parts, opt, in_hbm(vis_re), in_hbm(vis_im)), True)
        else:
            rows = (model_a, model_b, opt, vis_re, vis_im, ohq, ohp)
            (mid,) = iterate(rows + (everyone.reshape(S, 256), gains), False)
        low = lax.ppermute(mid, "ch", UP)
        high = lax.ppermute(mid, "ch", DOWN)
        if step + 1 < ITERS:
            gains, block = smooth(where, mid, low, high, True)
            everyone = lax.all_to_all(block, ("y", "z"), split_axis=0, concat_axis=0, tiled=True)
            everyone = lax.all_gather(everyone, "core", axis=0, tiled=True)
        else:
            (gains,) = smooth(where, mid, low, high, False)
    return gains.reshape(8, 2, ND, 16).transpose(3, 2, 1, 0).reshape(16, 2 * ND, 8)


def solution(mesh):
    split = Mesh(mesh.devices.reshape(4, 8, 2, 4), BL + ("ch",))
    in_specs = (
        P(None, None, None, "ch"),
        P(BL, "ch"),
        P(BL),
        P("ch", None, BL),
        P("ch", BL),
        P(None, BL),
        P(),
    )
    out_specs = P("ch", None, BL)
    return jax.shard_map(body, mesh=split, in_specs=in_specs, out_specs=out_specs, check_vma=False)
```

time: 221 us -> 171 us (0.77)
  waiting for transfers between devices: 51.9 us -> 23.3 us
  Pallas kernels: 60.5 us -> 39.6 us
  starting transfers between devices: 38 us -> 45.3 us
  local copies, waits for them, and re-layouts: 6.68 us -> 2.66 us
  other arithmetic: 3.6 us -> 0.08 us
    all_to_all x2, waiting for transfers between devices: 21.2 us -> 0.01 us  [exchange(): return lax.all_to_all(value, BL, split_axis=0, concat_axis=0, tiled=True)]
    all_gather x0 -> x3, blocking collectives: none -> 16.1 us  [body(): everyone = lax.all_gather(everyone, 'core', axis=0, tiled=True)]
    pallas_call x9 -> x15, Pallas kernels: 54.5 us -> 39.3 us  [the longest x4 13.5 us: iterate(): pl.pallas_call(iterate_kernel(first), out_shape=[jax.ShapeDtypeStruct((8,...]
    all_to_all x3, blocking collectives: 58.6 us -> 43.4 us  [body(): lax.all_to_all(block, ('y', 'z'), split_axis=0, concat_axis=0, tiled=True)]
    ppermute x14 -> x20, waiting for transfers between devices: 30.8 us -> 23.3 us  [the longest x2 7.58 us: last_legs(): chain_a = lax.ppermute(pair_sum(chain_a, next_a), 'ch', UP)]
    ppermute x14 -> x20, starting transfers between devices: 13.4 us -> 20 us  [the longest x2 5.4 us: last_legs(): chain_b = lax.ppermute(pair_sum(chain_b, prev_b), 'ch', DOWN)]
    pallas_call x4, Pallas kernels: 5.94 us -> 0.32 us  [smooth(): pl.pallas_call(smooth_kernel(spread), out_shape=shapes, in_specs=[smem, v...]
    convert_element_type x3 -> x1, other arithmetic: 2.93 us -> 0.01 us  [body(): solver_order.reshape(32, 2, 8).transpose(1, 0, 2).astype(F32).reshape(1, S)]
  transfers between devices with their start and end apart: 16 -> 22, of which waited for: 12 -> 14; matrix products, arithmetic and copies ran while one was open for 2% -> 0% of each run, Pallas kernels for 8% -> 13%
where the time goes in v2:
time: 171 us
  blocking collectives  59.5 us (35%)
  starting transfers between devices  45.3 us (26%)
  Pallas kernels  39.6 us (23%)
  waiting for transfers between devices  23.3 us (14%)
  local copies, waits for them, and re-layouts  2.66 us (2%)
    all_to_all x3, blocking collectives, body(): lax.all_to_all(block, ('y', 'z'), split_axis=0, concat_axis=0, tiled=True)  43.4 us
    all_to_all x2, starting transfers between devices, exchange(): return lax.all_to_all(value, BL, split_axis=0, concat_axis=0, tiled=True)  25.2 us
    all_gather x3, blocking collectives, body(): everyone = lax.all_gather(everyone, 'core', axis=0, tiled=True)  16.1 us
    pallas_call x4, Pallas kernels, iterate(): pl.pallas_call(iterate_kernel(first), out_shape=[jax.ShapeDtypeStruct((8,...  13.5 us
    pallas_call x2, Pallas kernels, late_degrid(): pl.pallas_call(late_kernel(jobs), out_shape=[jax.ShapeDtypeStruct((HALF,...  8.13 us
    ppermute x2, waiting for transfers between devices, last_legs(): chain_a = lax.ppermute(pair_sum(chain_a, next_a), 'ch', UP)  7.58 us
    pallas_call x2, Pallas kernels, degrid(): pl.pallas_call(degrid_kernel(count), out_shape=[half] * (2 * count) + [ta...  6.83 us
    ppermute x4, waiting for transfers between devices, body(): low = lax.ppermute(mid, 'ch', UP)  6.65 us
  transfers between devices with their start and end apart: 22, of which 14 were waited for; matrix products, arithmetic and copies ran while one was open for 0% of the time, Pallas kernels for 13%

profile of v2, /device:TPU:1, one launch (start us, length us, event | category | flops | bytes accessed | tf_op | source)
XLA Modules:
  0.0 170.5 jit_solution(17909501288033854340)
XLA Ops:
  0.0 0.7 copy-done.4
  0.7 4.2 %payload.1 = (bf16[64,24,256]{2,1,0:T(8,128)(2,1)}, bf16[1024,128]{1,0:T(8,128)(2,1)S(1)}) custom-call(s32[4]{0:T(128)S(1)} %copy-done.4, bf16[16,2,2048]{2,1,0:T(2,128)(2,1)} %obs_ref.1, s32[16,2048]{1,0:T(8,128)} %flag_ref.1, s32[2,2048]{1,0:T(2,128)} %pair_ref.1, bf16[64,32,256]{2,1,0:T(8,128)(2,1)} %bitcast.24), custom_call_target="tpu_custom_call" | custom-call | tf_op jit(solution)/shard_map/payload/pallas_call | solution.py:154
  5.0 13.1 %all-to-all-start.1 = ((bf16[64,24,256]{2,1,0:T(8,128)(2,1)}), bf16[64,24,256]{2,1,0:T(8,128)(2,1)S(1)}, u32[]{:S(2)}, u32[]{:S(2)}) async-start(bf16[64,24,256]{2,1,0:T(8,128)(2,1)} %get-tuple-element.50), calls=%async_computation.1 | async-start | bytes 1572864 | tf_op jit(solution)/shard_map/all_to_all | solution.py:371
  18.1 2.9 %shard_map.74 = (bf16[512,256]{1,0:T(8,128)(2,1)S(1)}, bf16[512,256]{1,0:T(8,128)(2,1)S(1)}, bf16[4,256,256]{2,1,0:T(8,128)(2,1)}) custom-call(s32[1]{0:T(128)} %bitcast.where_ref, s32[4]{0:T(128)S(1)} %copy-done.5, bf16[64,32,256]{2,1,0:T(8,128)(2,1)} %bitcast.25, bf16[4,64,16,256]{3,2,1,0:T(8,128)(2,1)} %refs_0_.3), custom_call_target="tpu_custom_call" | custom-call | tf_op jit(solution)/shard_map/pallas_call | solution.py:71
  21.0 1.2 collective-permute-start
  22.2 1.5 collective-permute-start.2
  23.7 4.0 %shard_map.73 = (bf16[512,256]{1,0:T(8,128)(2,1)S(1)}, bf16[512,256]{1,0:T(8,128)(2,1)S(1)}, bf16[512,256]{1,0:T(8,128)(2,1)S(1)}, bf16[512,256]{1,0:T(8,128)(2,...) custom-call(s32[1]{0:T(128)} %bitcast.where_ref, ...), custom_call_target="tpu_custom_call" | custom-call | tf_op jit(solution)/shard_map/pallas_call | solution.py:71
  27.6 1.3 collective-permute-start.4
  29.1 0.5 collective-permute-done.left_ref
  29.8 2.7 %collective-permute-start.3 = (bf16[512,256]{1,0:T(8,128)(2,1)S(1)}, bf16[512,256]{1,0:T(8,128)(2,1)S(1)}, u32[]{:S(2)}, u32[]{:S(2)}) collective-permute-start(bf16[512,256]{1,0:T(8,128)(2,1)S(1)} %pair.5), channel_id=1, source_target_pairs={{0,3},{1,0},{2,1},{3,2},{4,7},{5,4},{6,5},{7,6},{8,11},{9,8},{10,9... | collective-permute-start | bytes 786440 | tf_op jit(solution)/shard_map/ppermute | solution.py:366
  32.6 2.3 %collective-permute-done.4.near_a = bf16[512,256]{1,0:T(8,128)(2,1)S(1)} collective-permute-done((bf16[512,256]{1,0:T(8,128)(2,1)S(1)}, bf16[512,256]{1,0:T(8,128)(2,1)S(1)}, u32[]{:S(2)}, u32[]{:S(2)}) %collective-permute-start.4) | collective-permute-done | bytes 262176 | tf_op jit(solution)/shard_map/ppermute | solution.py:390
  34.8 1.8 %collective-permute-done.5.near_b = bf16[512,256]{1,0:T(8,128)(2,1)S(1)} collective-permute-done((bf16[512,256]{1,0:T(8,128)(2,1)S(1)}, bf16[512,256]{1,0:T(8,128)(2,1)S(1)}, u32[]{:S(2)}, u32[]{:S(2)}) %collective-permute-start.5) | collective-permute-done | bytes 262176 | tf_op jit(solution)/shard_map/ppermute | solution.py:391
  36.7 5.6 %collective-permute-done.1.chain_a = bf16[512,256]{1,0:T(8,128)(2,1)S(1)} collective-permute-done((bf16[512,256]{1,0:T(8,128)(2,1)S(1)}, bf16[512,256]{1,0:T(8,128)(2,1)S(1)}, u32[]{:S(2)}, u32[]{:S(2)}) %collective-permute-start.1) | collective-permute-done | bytes 262176 | tf_op jit(solution)/shard_map/ppermute | solution.py:365
  42.3 1.1 add.19
  43.4 12.1 %all-to-all-start = ((bf16[64,16,256]{2,1,0:T(8,128)(2,1)}), bf16[64,16,256]{2,1,0:T(8,128)(2,1)S(1)}, u32[]{:S(2)}, u32[]{:S(2)}) async-start(bf16[64,16,256]{2,1,0:T(8,128)(2,1)} %bitcast.2), calls=%async_computation | async-start | bytes 1048576 | tf_op jit(solution)/shard_map/all_to_all | solution.py:371
  55.5 4.1 %late.3 = (bf16[512,256]{1,0:T(8,128)(2,1)S(1)}, bf16[512,256]{1,0:T(8,128)(2,1)S(1)}, bf16[512,256]{1,0:T(8,128)(2,1)}, bf16[512,256]{1,0:T(8,128)(2,1)}) custom-call(bf16[64,24,256]{2,1,0:T(8,128)(2,1)S(1)} %all-to-all-done.1.pay_ref, bf16[4,256,256]{2,1,0:T(8,128)(2,1)} %get-tuple-element.56.refs_0_, bf16[4,256,256]{2,1,0:T(8,128)(2,1)} %get-tuple-element.52.refs_1_, ...), custom_call_target="tpu_custom_call" | custom-call | tf_op jit(solution)/shard_map/late/pallas_call | solution.py:112
  59.6 2.7 %collective-permute-start.8 = (bf16[512,256]{1,0:T(8,128)(2,1)S(1)}, bf16[512,256]{1,0:T(8,128)(2,1)S(1)}, u32[]{:S(2)}, u32[]{:S(2)}) collective-permute-start(bf16[512,256]{1,0:T(8,128)(2,1)S(1)} %get-tuple-element.59), channel_id=1, source_target_pairs={{0,3},{1,0},{2,1},{3,2},{4,7},{5,4},{6,5},{7,6},{8,11},{9,8},{10,9... | collective-permute-start | bytes 786440 | tf_op jit(solution)/shard_map/ppermute | solution.py:401
  62.2 1.4 collective-permute-start.11
  63.7 4.1 %late.2 = (bf16[512,256]{1,0:T(8,128)(2,1)S(1)}, bf16[512,256]{1,0:T(8,128)(2,1)S(1)}, bf16[512,256]{1,0:T(8,128)(2,1)}, bf16[512,256]{1,0:T(8,128)(2,1)}) custom-call(bf16[64,24,256]{2,1,0:T(8,128)(2,1)S(1)} %all-to-all-done.1.pay_ref, bf16[4,256,256]{2,1,0:T(8,128)(2,1)} %get-tuple-element.51.refs_0_.refs_2_, ...), custom_call_target="tpu_custom_call" | custom-call | tf_op jit(solution)/shard_map/late/pallas_call | solution.py:112
  68.2 0.8 pair.6
  68.9 0.8 pair.7
  69.7 2.7 %collective-permute-start.9 = (bf16[512,256]{1,0:T(8,128)(2,1)}, bf16[512,256]{1,0:T(8,128)(2,1)}, u32[]{:S(2)}, u32[]{:S(2)}) collective-permute-start(bf16[512,256]{1,0:T(8,128)(2,1)} %pair.7), channel_id=1, source_target_pairs={{0,3},{1,0},{2,1},{3,2},{4,7},{5,4},{6,5},{7,6},{8,11},{9,8},{10,9... | collective-permute-start | bytes 786440 | tf_op jit(solution)/shard_map/ppermute | solution.py:366
  72.8 3.8 %setup.1 = (bf16[2048,512]{1,0:T(8,128)(2,1)S(1)}, bf16[2048,128]{1,0:T(8,128)(2,1)S(1)}, bf16[16,2048]{1,0:T(8,128)(2,1)S(1)}, bf16[2048,128]{1,0:T(8,128)(2,1)...) custom-call(bf16[64,24,256]{2,1,0:T(8,128)(2,1)S(1)} %all-to-all-done.1.pay_ref, f32[1,512]{1,0:T(1,128)S(1)} %reshape.73.order_ref, ...), custom_call_target="tpu_custom_call" | custom-call | tf_op jit(solution)/shard_map/setup/pallas_call | solution.py:219
  76.6 0.8 copy-done.2
  77.4 2.0 %collective-permute-done.7.refs_3_ = bf16[512,256]{1,0:T(8,128)(2,1)} collective-permute-done((bf16[512,256]{1,0:T(8,128)(2,1)}, bf16[512,256]{1,0:T(8,128)(2,1)}, u32[]{:S(2)}, u32[]{:S(2)}) %collective-permute-start.7) | collective-permute-done | bytes 262176 | tf_op jit(solution)/shard_map/ppermute | solution.py:365
  79.4 4.7 %iterate0.1 = (f32[8,256]{1,0:T(8,128)S(1)}, bf16[1024,256]{1,0:T(8,128)(2,1)S(1)}) custom-call(bf16[1024,256]{1,0:T(8,128)(2,1)S(1)} %bitcast.17, bf16[512,256]{1,0:T(8,128)(2,1)} %get-tuple-element.54.refs_1_, bf16[512,256]{1,0:T(8,128)(2,1)} %get-tuple-element.55.refs_2_, bf16[512,256]{1,0:T(8,128)(2,1)} %collective-permute-done.7.refs_3_, ...), custom_call_target="tpu_custom_call" | custom-call | tf_op jit(solution)/shard_map/iterate0/pallas_call | solution.py:287
  84.1 1.6 collective-permute-start.13
  85.7 0.9 collective-permute-done.13.high_ref
  86.6 2.8 %collective-permute-done.12.low_ref = f32[8,256]{1,0:T(8,128)S(1)} collective-permute-done((f32[8,256]{1,0:T(8,128)S(1)}, f32[8,256]{1,0:T(8,128)S(1)}, u32[]{:S(2)}, u32[]{:S(2)}) %collective-permute-start.12) | collective-permute-done | bytes 8224 | tf_op jit(solution)/shard_map/ppermute | solution.py:418
  89.5 18.5 %all_to_all.25 = bf16[32,8,256]{2,1,0:T(8,128)(2,1)S(1)} all-to-all(bf16[32,8,256]{2,1,0:T(8,128)(2,1)S(1)} %get-tuple-element.71), channel_id=1, replica_groups=mesh['y'=4,'z'=8,'core'=2,'ch'=4] {'y','z'}, dimensions={0} | all-to-all | bytes 262144 | tf_op jit(solution)/shard_map/all_to_all | solution.py:422
  108.0 6.9 %all_gather.9 = bf16[64,8,256]{2,1,0:T(8,128)(2,1)S(1)} all-gather(bf16[32,8,256]{2,1,0:T(8,128)(2,1)S(1)} %all_to_all.25), channel_id=1, replica_groups=mesh['y'=4,'z'=8,'core'=2,'ch'=4] {'core'}, dimensions={0}, use_global_device_ids=true | all-gather | bytes 393216 | tf_op jit(solution)/shard_map/all_gather | solution.py:423
  114.9 2.9 %iterate.3.mid_ref = f32[8,256]{1,0:T(8,128)S(1)} custom-call(bf16[1024,256]{1,0:T(8,128)(2,1)S(1)} %bitcast.18, bf16[1024,256]{1,0:T(8,128)(2,1)S(1)} %get-tuple-element.67.refs_1_, bf16[16,2048]{1,0:T(8,128)(2,1)S(1)} %get-tuple-element.64.refs_8_.refs_2_, bf16[2048,128]{1,0:T(8,128)(2,1)S(1)} %copy-done, bf16[2048,128]{1,0:T(8,128)(2,1)S(1)} %copy-done.1, ...), custom_call_target="tpu_custom_call" | custom-call | tf_op jit(solution)/shard_map/iterate/pallas_call | solution.py:287
  118.1 1.5 collective-permute-start.14
  119.5 1.0 collective-permute-done.15.high_ref
  120.6 1.3 collective-permute-done.14.low_ref
  122.0 12.5 %all_to_all.26 = bf16[32,8,256]{2,1,0:T(8,128)(2,1)S(1)} all-to-all(bf16[32,8,256]{2,1,0:T(8,128)(2,1)S(1)} %get-tuple-element.73), channel_id=1, replica_groups=mesh['y'=4,'z'=8,'core'=2,'ch'=4] {'y','z'}, dimensions={0} | all-to-all | bytes 262144 | tf_op jit(solution)/shard_map/all_to_all | solution.py:422
  134.5 4.6 %all_gather.10 = bf16[64,8,256]{2,1,0:T(8,128)(2,1)S(1)} all-gather(bf16[32,8,256]{2,1,0:T(8,128)(2,1)S(1)} %all_to_all.26), channel_id=1, replica_groups=mesh['y'=4,'z'=8,'core'=2,'ch'=4] {'core'}, dimensions={0}, use_global_device_ids=true | all-gather | bytes 393216 | tf_op jit(solution)/shard_map/all_gather | solution.py:423
  139.1 2.9 %iterate.4.mid_ref = f32[8,256]{1,0:T(8,128)S(1)} custom-call(bf16[1024,256]{1,0:T(8,128)(2,1)S(1)} %bitcast.19, bf16[1024,256]{1,0:T(8,128)(2,1)S(1)} %get-tuple-element.67.refs_1_, bf16[16,2048]{1,0:T(8,128)(2,1)S(1)} %get-tuple-element.64.refs_8_.refs_2_, bf16[2048,128]{1,0:T(8,128)(2,1)S(1)} %copy-done, bf16[2048,128]{1,0:T(8,128)(2,1)S(1)} %copy-done.1, ...), custom_call_target="tpu_custom_call" | custom-call | tf_op jit(solution)/shard_map/iterate/pallas_call | solution.py:287
  142.0 1.5 collective-permute-start.16
  143.5 1.0 collective-permute-done.17.high_ref
  144.5 1.3 collective-permute-done.16.low_ref
  145.9 12.4 %all_to_all.27 = bf16[32,8,256]{2,1,0:T(8,128)(2,1)S(1)} all-to-all(bf16[32,8,256]{2,1,0:T(8,128)(2,1)S(1)} %get-tuple-element.75), channel_id=1, replica_groups=mesh['y'=4,'z'=8,'core'=2,'ch'=4] {'y','z'}, dimensions={0} | all-to-all | bytes 262144 | tf_op jit(solution)/shard_map/all_to_all | solution.py:422
  158.3 4.6 %all_gather.11 = bf16[64,8,256]{2,1,0:T(8,128)(2,1)S(1)} all-gather(bf16[32,8,256]{2,1,0:T(8,128)(2,1)S(1)} %all_to_all.27), channel_id=1, replica_groups=mesh['y'=4,'z'=8,'core'=2,'ch'=4] {'core'}, dimensions={0}, use_global_device_ids=true | all-gather | bytes 393216 | tf_op jit(solution)/shard_map/all_gather | solution.py:423
  162.9 2.9 %iterate.5.mid_ref = f32[8,256]{1,0:T(8,128)S(1)} custom-call(bf16[1024,256]{1,0:T(8,128)(2,1)S(1)} %bitcast.20, bf16[1024,256]{1,0:T(8,128)(2,1)S(1)} %get-tuple-element.67.refs_1_, bf16[16,2048]{1,0:T(8,128)(2,1)S(1)} %get-tuple-element.64.refs_8_.refs_2_, bf16[2048,128]{1,0:T(8,128)(2,1)S(1)} %copy-done, bf16[2048,128]{1,0:T(8,128)(2,1)S(1)} %copy-done.1, ...), custom_call_target="tpu_custom_call" | custom-call | tf_op jit(solution)/shard_map/iterate/pallas_call | solution.py:287
  165.8 1.5 collective-permute-start.18
  167.3 1.0 collective-permute-done.19.high_ref
  168.3 1.3 collective-permute-done.18.low_ref
  169.8 0.7 copy.14
  (45 shorter events, 1.9 us)
Async XLA Ops:
  0.0 18.1 %copy-start.5 = (s32[4]{0:T(128)S(1)}, s32[4]{0:T(128)}, u32[]{:S(2)}) copy-start(s32[4]{0:T(128)} %tile_ref.5) | copy-start | bytes 52
  0.0 0.7 copy-start.4
  5.0 38.4 %all-to-all-start.1 = ((bf16[64,24,256]{2,1,0:T(8,128)(2,1)}), bf16[64,24,256]{2,1,0:T(8,128)(2,1)S(1)}, u32[]{:S(2)}, u32[]{:S(2)}) async-start(bf16[64,24,256]{2,1,0:T(8,128)(2,1)} %get-tuple-element.50), calls=%async_computation.1 | async-start | bytes 1572864 | tf_op jit(solution)/shard_map/all_to_all | solution.py:371
  21.0 8.6 %collective-permute-start = (bf16[512,256]{1,0:T(8,128)(2,1)S(1)}, bf16[512,256]{1,0:T(8,128)(2,1)S(1)}, u32[]{:S(2)}, u32[]{:S(2)}) collective-permute-start(bf16[512,256]{1,0:T(8,128)(2,1)S(1)} %get-tuple-element.43), channel_id=1, source_target_pairs={{0,1},{1,2},{2,3},{3,0},{4,5},{5,6},{6,7},{7,4},{8,9},{9,10},{10,1... | collective-permute-start | bytes 786440 | tf_op jit(solution)/shard_map/ppermute | solution.py:385
  22.2 7.6 %collective-permute-start.2 = (bf16[512,256]{1,0:T(8,128)(2,1)S(1)}, bf16[512,256]{1,0:T(8,128)(2,1)S(1)}, u32[]{:S(2)}, u32[]{:S(2)}) collective-permute-start(bf16[512,256]{1,0:T(8,128)(2,1)S(1)} %get-tuple-element.45), channel_id=1, source_target_pairs={{0,3},{1,0},{2,1},{3,2},{4,7},{5,4},{6,5},{7,6},{8,11},{9,8},{10,9... | collective-permute-start | bytes 786440 | tf_op jit(solution)/shard_map/ppermute | solution.py:386
  27.6 7.2 %collective-permute-start.4 = (bf16[512,256]{1,0:T(8,128)(2,1)S(1)}, bf16[512,256]{1,0:T(8,128)(2,1)S(1)}, u32[]{:S(2)}, u32[]{:S(2)}) collective-permute-start(bf16[512,256]{1,0:T(8,128)(2,1)S(1)} %get-tuple-element.47), channel_id=1, source_target_pairs={{0,3},{1,0},{2,1},{3,2},{4,7},{5,4},{6,5},{7,6},{8,11},{9,8},{10,9... | collective-permute-start | bytes 786440 | tf_op jit(solution)/shard_map/ppermute | solution.py:390
  28.9 7.8 %collective-permute-start.5 = (bf16[512,256]{1,0:T(8,128)(2,1)S(1)}, bf16[512,256]{1,0:T(8,128)(2,1)S(1)}, u32[]{:S(2)}, u32[]{:S(2)}) collective-permute-start(bf16[512,256]{1,0:T(8,128)(2,1)S(1)} %get-tuple-element.48), channel_id=1, source_target_pairs={{0,1},{1,2},{2,3},{3,0},{4,5},{5,6},{6,7},{7,4},{8,9},{9,10},{10,1... | collective-permute-start | bytes 786440 | tf_op jit(solution)/shard_map/ppermute | solution.py:391
  29.7 12.6 %collective-permute-start.1 = (bf16[512,256]{1,0:T(8,128)(2,1)S(1)}, bf16[512,256]{1,0:T(8,128)(2,1)S(1)}, u32[]{:S(2)}, u32[]{:S(2)}) collective-permute-start(bf16[512,256]{1,0:T(8,128)(2,1)S(1)} %pair.4), channel_id=1, source_target_pairs={{0,1},{1,2},{2,3},{3,0},{4,5},{5,6},{6,7},{7,4},{8,9},{9,10},{10,1... | collective-permute-start | bytes 786440 | tf_op jit(solution)/shard_map/ppermute | solution.py:365
  29.8 12.5 %collective-permute-start.3 = (bf16[512,256]{1,0:T(8,128)(2,1)S(1)}, bf16[512,256]{1,0:T(8,128)(2,1)S(1)}, u32[]{:S(2)}, u32[]{:S(2)}) collective-permute-start(bf16[512,256]{1,0:T(8,128)(2,1)S(1)} %pair.5), channel_id=1, source_target_pairs={{0,3},{1,0},{2,1},{3,2},{4,7},{5,4},{6,5},{7,6},{8,11},{9,8},{10,9... | collective-permute-start | bytes 786440 | tf_op jit(solution)/shard_map/ppermute | solution.py:366
  43.4 34.0 %all-to-all-start = ((bf16[64,16,256]{2,1,0:T(8,128)(2,1)}), bf16[64,16,256]{2,1,0:T(8,128)(2,1)S(1)}, u32[]{:S(2)}, u32[]{:S(2)}) async-start(bf16[64,16,256]{2,1,0:T(8,128)(2,1)} %bitcast.2), calls=%async_computation | async-start | bytes 1048576 | tf_op jit(solution)/shard_map/all_to_all | solution.py:371
  59.5 12.9 %copy-start.6 = (s32[512]{0:T(512)S(1)}, s32[512]{0:T(512)}, u32[]{:S(2)}) copy-start(s32[512]{0:T(512)} %param.13) | copy-start | bytes 6148
  59.6 8.6 %collective-permute-start.6 = (bf16[512,256]{1,0:T(8,128)(2,1)S(1)}, bf16[512,256]{1,0:T(8,128)(2,1)S(1)}, u32[]{:S(2)}, u32[]{:S(2)}) collective-permute-start(bf16[512,256]{1,0:T(8,128)(2,1)S(1)} %get-tuple-element.57), channel_id=1, source_target_pairs={{0,1},{1,2},{2,3},{3,0},{4,5},{5,6},{6,7},{7,4},{8,9},{9,10},{10,1... | collective-permute-start | bytes 786440 | tf_op jit(solution)/shard_map/ppermute | solution.py:400
  59.6 9.4 %collective-permute-start.8 = (bf16[512,256]{1,0:T(8,128)(2,1)S(1)}, bf16[512,256]{1,0:T(8,128)(2,1)S(1)}, u32[]{:S(2)}, u32[]{:S(2)}) collective-permute-start(bf16[512,256]{1,0:T(8,128)(2,1)S(1)} %get-tuple-element.59), channel_id=1, source_target_pairs={{0,3},{1,0},{2,1},{3,2},{4,7},{5,4},{6,5},{7,6},{8,11},{9,8},{10,9... | collective-permute-start | bytes 786440 | tf_op jit(solution)/shard_map/ppermute | solution.py:401
  62.2 15.2 %collective-permute-start.10 = (bf16[512,256]{1,0:T(8,128)(2,1)}, bf16[512,256]{1,0:T(8,128)(2,1)}, u32[]{:S(2)}, u32[]{:S(2)}) collective-permute-start(bf16[512,256]{1,0:T(8,128)(2,1)} %get-tuple-element.61), channel_id=1, source_target_pairs={{0,3},{1,0},{2,1},{3,2},{4,7},{5,4},{6,5},{7,6},{8,11},{9,8},{10,9... | collective-permute-start | bytes 786440 | tf_op jit(solution)/shard_map/ppermute | solution.py:402
  62.2 15.2 %collective-permute-start.11 = (bf16[512,256]{1,0:T(8,128)(2,1)}, bf16[512,256]{1,0:T(8,128)(2,1)}, u32[]{:S(2)}, u32[]{:S(2)}) collective-permute-start(bf16[512,256]{1,0:T(8,128)(2,1)} %get-tuple-element.62), channel_id=1, source_target_pairs={{0,1},{1,2},{2,3},{3,0},{4,5},{5,6},{6,7},{7,4},{8,9},{9,10},{10,1... | collective-permute-start | bytes 786440 | tf_op jit(solution)/shard_map/ppermute | solution.py:403
  68.9 10.5 %collective-permute-start.7 = (bf16[512,256]{1,0:T(8,128)(2,1)}, bf16[512,256]{1,0:T(8,128)(2,1)}, u32[]{:S(2)}, u32[]{:S(2)}) collective-permute-start(bf16[512,256]{1,0:T(8,128)(2,1)} %pair.6), channel_id=1, source_target_pairs={{0,1},{1,2},{2,3},{3,0},{4,5},{5,6},{6,7},{7,4},{8,9},{9,10},{10,1... | collective-permute-start | bytes 786440 | tf_op jit(solution)/shard_map/ppermute | solution.py:365
  69.7 9.7 %collective-permute-start.9 = (bf16[512,256]{1,0:T(8,128)(2,1)}, bf16[512,256]{1,0:T(8,128)(2,1)}, u32[]{:S(2)}, u32[]{:S(2)}) collective-permute-start(bf16[512,256]{1,0:T(8,128)(2,1)} %pair.7), channel_id=1, source_target_pairs={{0,3},{1,0},{2,1},{3,2},{4,7},{5,4},{6,5},{7,6},{8,11},{9,8},{10,9... | collective-permute-start | bytes 786440 | tf_op jit(solution)/shard_map/ppermute | solution.py:366
  76.6 0.8 copy-start.2
  77.4 37.5 %copy-start = (bf16[2048,128]{1,0:T(8,128)(2,1)S(1)}, bf16[2048,128]{1,0:T(8,128)(2,1)}, u32[]{:S(2)}) copy-start(bf16[2048,128]{1,0:T(8,128)(2,1)} %get-tuple-element.65.refs_9_.refs_3_) | copy-start | bytes 1572868
  77.4 37.5 %copy-start.1 = (bf16[2048,128]{1,0:T(8,128)(2,1)S(1)}, bf16[2048,128]{1,0:T(8,128)(2,1)}, u32[]{:S(2)}) copy-start(bf16[2048,128]{1,0:T(8,128)(2,1)} %get-tuple-element.66.refs_10_.refs_4_) | copy-start | bytes 1572868
  77.4 37.5 %copy-start.3 = (bf16[2048,128]{1,0:T(8,128)(2,1)S(1)}, bf16[2048,128]{1,0:T(8,128)(2,1)}, u32[]{:S(2)}) copy-start(bf16[2048,128]{1,0:T(8,128)(2,1)} %copy-done.2) | copy-start | bytes 1572868
  84.1 2.5 %collective-permute-start.13 = (f32[8,256]{1,0:T(8,128)S(1)}, f32[8,256]{1,0:T(8,128)S(1)}, u32[]{:S(2)}, u32[]{:S(2)}) collective-permute-start(f32[8,256]{1,0:T(8,128)S(1)} %get-tuple-element.70.mid_ref), channel_id=1, source_target_pairs={{0,3},{1,0},{2,1},{3,2},{4,7},{5,4},{6,5},{7,6},{8,11},{9,8},{10,9... | collective-permute-start | bytes 24584 | tf_op jit(solution)/shard_map/ppermute | solution.py:419
  85.7 3.7 %collective-permute-start.12 = (f32[8,256]{1,0:T(8,128)S(1)}, f32[8,256]{1,0:T(8,128)S(1)}, u32[]{:S(2)}, u32[]{:S(2)}) collective-permute-start(f32[8,256]{1,0:T(8,128)S(1)} %get-tuple-element.70.mid_ref), channel_id=1, source_target_pairs={{0,1},{1,2},{2,3},{3,0},{4,5},{5,6},{6,7},{7,4},{8,9},{9,10},{10,1... | collective-permute-start | bytes 24584 | tf_op jit(solution)/shard_map/ppermute | solution.py:418
  117.9 2.7 %collective-permute-start.15 = (f32[8,256]{1,0:T(8,128)S(1)}, f32[8,256]{1,0:T(8,128)S(1)}, u32[]{:S(2)}, u32[]{:S(2)}) collective-permute-start(f32[8,256]{1,0:T(8,128)S(1)} %iterate.3.mid_ref), channel_id=1, source_target_pairs={{0,3},{1,0},{2,1},{3,2},{4,7},{5,4},{6,5},{7,6},{8,11},{9,8},{10,9... | collective-permute-start | bytes 24584 | tf_op jit(solution)/shard_map/ppermute | solution.py:419
  118.1 3.8 %collective-permute-start.14 = (f32[8,256]{1,0:T(8,128)S(1)}, f32[8,256]{1,0:T(8,128)S(1)}, u32[]{:S(2)}, u32[]{:S(2)}) collective-permute-start(f32[8,256]{1,0:T(8,128)S(1)} %iterate.3.mid_ref), channel_id=1, source_target_pairs={{0,1},{1,2},{2,3},{3,0},{4,5},{5,6},{6,7},{7,4},{8,9},{9,10},{10,1... | collective-permute-start | bytes 24584 | tf_op jit(solution)/shard_map/ppermute | solution.py:418
  142.0 2.5 %collective-permute-start.17 = (f32[8,256]{1,0:T(8,128)S(1)}, f32[8,256]{1,0:T(8,128)S(1)}, u32[]{:S(2)}, u32[]{:S(2)}) collective-permute-start(f32[8,256]{1,0:T(8,128)S(1)} %iterate.4.mid_ref), channel_id=1, source_target_pairs={{0,3},{1,0},{2,1},{3,2},{4,7},{5,4},{6,5},{7,6},{8,11},{9,8},{10,9... | collective-permute-start | bytes 24584 | tf_op jit(solution)/shard_map/ppermute | solution.py:419
  142.0 3.8 %collective-permute-start.16 = (f32[8,256]{1,0:T(8,128)S(1)}, f32[8,256]{1,0:T(8,128)S(1)}, u32[]{:S(2)}, u32[]{:S(2)}) collective-permute-start(f32[8,256]{1,0:T(8,128)S(1)} %iterate.4.mid_ref), channel_id=1, source_target_pairs={{0,1},{1,2},{2,3},{3,0},{4,5},{5,6},{6,7},{7,4},{8,9},{9,10},{10,1... | collective-permute-start | bytes 24584 | tf_op jit(solution)/shard_map/ppermute | solution.py:418
  165.8 2.5 %collective-permute-start.19 = (f32[8,256]{1,0:T(8,128)S(1)}, f32[8,256]{1,0:T(8,128)S(1)}, u32[]{:S(2)}, u32[]{:S(2)}) collective-permute-start(f32[8,256]{1,0:T(8,128)S(1)} %iterate.5.mid_ref), channel_id=1, source_target_pairs={{0,3},{1,0},{2,1},{3,2},{4,7},{5,4},{6,5},{7,6},{8,11},{9,8},{10,9... | collective-permute-start | bytes 24584 | tf_op jit(solution)/shard_map/ppermute | solution.py:419
  165.8 3.8 %collective-permute-start.18 = (f32[8,256]{1,0:T(8,128)S(1)}, f32[8,256]{1,0:T(8,128)S(1)}, u32[]{:S(2)}, u32[]{:S(2)}) collective-permute-start(f32[8,256]{1,0:T(8,128)S(1)} %iterate.5.mid_ref), channel_id=1, source_target_pairs={{0,1},{1,2},{2,3},{3,0},{4,5},{5,6},{6,7},{7,4},{8,9},{9,10},{10,1... | collective-permute-start | bytes 24584 | tf_op jit(solution)/shard_map/ppermute | solution.py:418

commit v3 on v2

--- a/solution.py
+++ b/solution.py
@@ -50,12 +50,14 @@
         order = lane_order()
         for index in range(count):
             for tile in range(4):
-                tables[index][tile] = nn(order, facets[index][tile].reshape(256, 256)).astype(BF16)
+                columns = slice(tile * 256, (tile + 1) * 256)
+                tables[index][:, columns] = nn(order, facets[index][tile].reshape(256, 256)).astype(BF16)
         for block in range(4):
             rows = kern_ref[block * 16 : (block + 1) * 16].reshape(256, 256)
             place = slice((block % 2) * 256, (block % 2) * 256 + 256)
+            columns = pl.ds(pl.multiple_of(tile_ref[block] * 256, 256), 256)
             for index in range(count):
-                outs[2 * index + block // 2][place, :] = nt(rows, tables[index][tile_ref[block]]).astype(BF16)
+                outs[2 * index + block // 2][place, :] = nt(rows, tables[index][:, columns]).astype(BF16)
 
     return run
 
@@ -67,7 +69,7 @@
         return pl.BlockSpec((4, 16, 16, 256), lambda i, where, tile: (0, (where[0] + shift) & 3, 0, 0))
 
     half = jax.ShapeDtypeStruct((HALF, 256), BF16)
-    table = pltpu.HBM((4, 256, 256), BF16)
+    table = pltpu.HBM((256, 1024), BF16)
     return pl.pallas_call(
         degrid_kernel(count),
         out_shape=[half] * (2 * count) + [table] * count,
@@ -75,50 +77,73 @@
             num_scalar_prefetch=2,
             grid=(1,),
             in_specs=[full((64, 16, 256))] + [facet_spec(g) for g in groups],
-            out_specs=[full((HALF, 256))] * (2 * count) + [full((4, 256, 256))] * count,
+            out_specs=[full((HALF, 256))] * (2 * count) + [full((256, 1024))] * count,
         ),
         compiler_params=SMALL,
     )(where, tile_of, in_hbm(kernel), *([in_hbm(facet_grid)] * count))
 
 
 def late_kernel(jobs):
-    def run(pay_ref, *refs):
-        tables, outs = refs[:3], refs[3:]
+    def run(pay_ref, first_ref, second_ref, third_ref, *refs):
+        outs, (lhs_ref, table_ref, sems) = refs[:-3], refs[-3:]
+        loads = [
+            pltpu.make_async_copy(source, table_ref.at[index], sems.at[index])
+            for index, source in enumerate((first_ref, second_ref, third_ref))
+        ]
+        for load in loads:
+            load.start()
         weight = (iota((LANES, 256), 0) == 52).astype(F32).astype(BF16)
+
+        def mask(block, carry):
+            segments = pl.ds(block * 16, 16)
+            rows = pay_ref[segments, :16, :].reshape(256, 256)
+            small = pay_ref[segments, 16:24, 128:].astype(F32).reshape(128, LANES)
+            early = nn(small.astype(BF16), weight).reshape(16, 8, 256)
+            late = nn(pltpu.roll(small, 64, 1).astype(BF16), weight).reshape(16, 8, 256)
+            tile = jnp.concatenate([early, late], axis=1).reshape(256, 256)
+            place = pl.ds(pl.multiple_of(block * 256, 256), 256)
+            for t in range(4):
+                lhs_ref[place, t * 256 : (t + 1) * 256] = rows * (tile == float(t)).astype(F32).astype(BF16)
+            return carry
+
+        lax.fori_loop(0, 4, mask, 0, unroll=2)
+        for load in loads:
+            load.wait()
         for half in range(2):
-
-            def step(block, carry, half=half):
-                segments = pl.ds(half * 32 + block * 16, 16)
-                rows = pay_ref[segments, :16, :].reshape(256, 256)
-                small = pay_ref[segments, 16:24, 128:].astype(F32).reshape(128, LANES)
-                early = nn(small.astype(BF16), weight).reshape(16, 8, 256)
-                late = nn(pltpu.roll(small, 64, 1).astype(BF16), weight).reshape(16, 8, 256)
-                tile = jnp.concatenate([early, late], axis=1).reshape(256, 256)
-                masked = [rows * (tile == float(t)).astype(F32).astype(BF16) for t in range(4)]
-                place = pl.ds(pl.multiple_of(block * 256, 256), 256)
-                for index, out in jobs[half]:
-                    total = nt(masked[0], tables[index][0])
-                    for t in range(1, 4):
-                        total = total + nt(masked[t], tables[index][t])
-                    outs[out][place, :] = total.astype(BF16)
-                return carry
-
-            lax.fori_loop(0, 2, step, 0, unroll=2)
+            for index, out, start in jobs[half]:
+
+                def step(block, carry, half=half, index=index, out=out, start=start):
+                    source = pl.ds(pl.multiple_of(half * 512 + block * 256, 256), 256)
+                    place = pl.ds(pl.multiple_of(start + block * 256, 256), 256)
+                    outs[out][place, :] = nt(lhs_ref[source, :], table_ref[index]).astype(BF16)
+                    return carry
+
+                lax.fori_loop(0, 2, step, 0, unroll=2)
 
     return run
 
 
-def late_degrid(payload, tables, jobs, last):
+def late_degrid(payload, tables, jobs, shapes):
+    vmem = pl.BlockSpec(memory_space=pltpu.VMEM)
+    anywhere = pl.BlockSpec(memory_space=pl.ANY)
     return pl.pallas_call(
         late_kernel(jobs),
-        out_shape=[jax.ShapeDtypeStruct((HALF, 256), BF16)] * 2 + [last] * 2,
+        out_shape=shapes,
+        in_specs=[vmem, anywhere, anywhere, anywhere],
+        out_specs=[vmem] * len(shapes),
+        scratch_shapes=[
+            pltpu.VMEM((1024, 1024), BF16),
+            pltpu.VMEM((3, 256, 1024), BF16),
+            pltpu.SemaphoreType.DMA((3,)),
+        ],
         compiler_params=SMALL,
         name="late",
     )(payload, *[in_hbm(table) for table in tables])
 
 
-def payload_kernel(tile_ref, obs_ref, flag_ref, pair_ref, kern_ref, out_ref, kept_ref, stacked_ref):
-    out_ref[:, :16, :] = kern_ref[...]
+def payload_kernel(tile_ref, obs_ref, flag_ref, pair_ref, kern_ref, out_ref, kept_ref, stacked_ref, sem):
+    bulk = pltpu.make_async_copy(kern_ref.at[:, 16:32, :], out_ref.at[:, 0:16, :], sem)
+    bulk.start()
     kept = (1 - flag_ref[...]).astype(F32)
     pair = pair_ref[...]
     high = (pair >> 3).astype(F32)
@@ -148,6 +173,7 @@
         return carry
 
     lax.fori_loop(0, ROWS // 128, step, 0, unroll=4)
+    bulk.wait()
 
 
 def make_payload(tile_of, observed, flags, pairs, kernel):
@@ -161,10 +187,10 @@
                 full((16, 2, ROWS)),
                 full((16, ROWS)),
                 full((2, ROWS)),
-                pl.BlockSpec((64, 16, 256), lambda i, tile: (0, 1, 0)),
+                pl.BlockSpec(memory_space=pl.ANY),
             ],
             out_specs=[full((64, 24, 256)), full((1024, LANES))],
-            scratch_shapes=[pltpu.VMEM((LANES, ROWS), F32)],
+            scratch_shapes=[pltpu.VMEM((LANES, ROWS), F32), pltpu.SemaphoreType.DMA],
         ),
         compiler_params=SMALL,
         name="payload",
@@ -209,8 +235,8 @@
 
 def make_setup(payload, order, own):
     shapes = [
-        jax.ShapeDtypeStruct((ROWS, S), BF16),
-        jax.ShapeDtypeStruct((ROWS, LANES), BF16),
+        pltpu.HBM((ROWS, S), BF16),
+        pltpu.HBM((ROWS, LANES), BF16),
         jax.ShapeDtypeStruct((16, ROWS), BF16),
         pltpu.HBM((ROWS, LANES), BF16),
         pltpu.HBM((ROWS, LANES), BF16),
@@ -228,16 +254,39 @@
 def iterate_kernel(first):
     def run(*refs):
         if first:
-            model_a, *parts, opt_ref, vre_ref, vim_ref, out_ref, model_b, terms_ref = refs
-            add_kernel(*parts, model_b)
+            model_a, chain_a, chain_b, opt_ref, *sources = refs[:11]
+            out_ref, model_b, terms_ref, vre_ref, vim_ref, kept_ref, own_a, own_b, near_a, near_b, sems = refs[11:]
+            vre_source, vim_source, kept_source, a_source, b_source, low_source, high_source = sources
+            early, late = slice(0, 1024), slice(1024, 2048)
+            moves = [
+                (vre_source.at[early], vre_ref.at[early]),
+                (vim_source.at[early], vim_ref.at[early]),
+                (kept_source, kept_ref),
+                (a_source, own_a),
+                (b_source, own_b),
+                (high_source.at[HALF:], near_a),
+                (low_source.at[HALF:], near_b),
+                (vre_source.at[late], vre_ref.at[late]),
+                (vim_source.at[late], vim_ref.at[late]),
+            ]
+            moves = [pltpu.make_async_copy(*move, sems.at[index]) for index, move in enumerate(moves)]
+            for move in moves:
+                move.start()
         else:
-            model_a, model_b, opt_ref, vre_ref, vim_ref, ohq_ref, ohp_ref, all_ref, own_ref, out_ref, terms_ref = refs
-            all_gains = all_ref[...]
+            model_a, model_b, opt_ref, vre_ref, vim_ref, ohq_ref, ohp_ref, here_ref, there_ref, own_ref, out_ref, terms_ref = refs
+            all_gains = jnp.concatenate([here_ref[...], there_ref[...]], axis=0)
             own = own_ref[...]
             high = own.astype(BF16).astype(F32)
             near_gains = jnp.concatenate([high, own - high, jnp.zeros((LANES - 16, 256), F32)], axis=0).astype(BF16)
 
         for i in range(ROWS // CHUNK):
+            if first and i == 0:
+                moves[0].wait()
+                moves[1].wait()
+            if first and i == 4:
+                for move in moves[2:]:
+                    move.wait()
+                add_kernel(own_a, own_b, chain_a, chain_b, near_a, near_b, kept_ref, model_b)
             rows = slice(i * CHUNK, (i + 1) * CHUNK)
             model = (model_a if i < 4 else model_b)[(i % 4) * CHUNK : (i % 4 + 1) * CHUNK, :].astype(F32)
             model_re, model_im = model[:, :128], model[:, 128:]
@@ -284,10 +333,18 @@
 
 
 def iterate(args, first):
+    vmem = pl.BlockSpec(memory_space=pltpu.VMEM)
+    anywhere = pl.BlockSpec(memory_space=pl.ANY)
+    scratch = [pltpu.VMEM((ROWS, 768), BF16)]
+    if first:
+        scratch += [pltpu.VMEM((ROWS, LANES), BF16)] * 2 + [pltpu.VMEM((1024, LANES), BF16)]
+        scratch += [pltpu.VMEM((HALF, 256), BF16)] * 4 + [pltpu.SemaphoreType.DMA((9,))]
     return pl.pallas_call(
         iterate_kernel(first),
         out_shape=[jax.ShapeDtypeStruct((8, 256), F32)] + [jax.ShapeDtypeStruct((1024, 256), BF16)] * first,
-        scratch_shapes=[pltpu.VMEM((ROWS, 768), BF16)],
+        in_specs=[vmem] * 4 + [anywhere] * 7 if first else [vmem] * len(args),
+        out_specs=[vmem] * (2 if first else 1),
+        scratch_shapes=scratch,
         compiler_params=SMALL,
         name="iterate0" if first else "iterate",
     )(*args)
@@ -335,9 +392,16 @@
 
 
 def pair_sum(left, right):
-    return pl.pallas_call(
-        pair_kernel, out_shape=jax.ShapeDtypeStruct((HALF, 256), BF16), compiler_params=SMALL, name="pair"
-    )(left, right)
+    block = pl.BlockSpec((HALF, 256), lambda i: (0, 0))
+    return pl.pallas_call(
+        pair_kernel,
+        out_shape=jax.ShapeDtypeStruct((HALF, 256), BF16),
+        grid=(1,),
+        in_specs=[block, block],
+        out_specs=block,
+        compiler_params=SMALL,
+        name="pair",
+    )(in_hbm(left) if left.shape[0] > HALF else left, right)
 
 
 def add_kernel(own_a, own_b, chain_a, chain_b, near_a, near_b, kept_ref, out_ref):
@@ -379,7 +443,8 @@
 
     mine = lax.dynamic_slice(solver_order, (8 * lax.axis_index(BL),), (8,))
     own_row = jnp.concatenate([mine, mine, jnp.full((LANES - 16,), -1, jnp.int32)]).astype(F32).reshape(1, LANES)
-    order_row = solver_order.reshape(32, 2, 8).transpose(1, 0, 2).astype(F32).reshape(1, S)
+    halves = solver_order.reshape(32, 2, 8).transpose(1, 0, 2).astype(F32).reshape(2, S // 2)
+    order_row = jnp.where(lax.axis_index("core") == 0, halves, halves[::-1]).reshape(1, S)
 
     far_a, far_b, table2 = degrid(where, tile_of, kernel, facet_grid, (2,))
     chain_a = lax.ppermute(far_a, "ch", UP)
@@ -392,35 +457,38 @@
     legs = last_legs(chain_a, chain_b, direct_a, direct_b, next_a, prev_b)
     model_a = total(own_a, own_b, *legs, kept_a)
 
-    near = jax.ShapeDtypeStruct((HALF, 256), BF16)
+    half = jax.ShapeDtypeStruct((HALF, 256), BF16)
     away = pltpu.HBM((HALF, 256), BF16)
-    far_a, far_b, prev_a, next_b = late_degrid(
-        arrived, (table2, table3, table1), (((0, 0), (1, 2)), ((0, 1), (2, 3))), near
+    whole = pltpu.HBM((2 * HALF, 256), BF16)
+    going_up, going_down = late_degrid(
+        arrived,
+        (table2, table3, table1),
+        (((0, 0, 0), (1, 1, HALF)), ((0, 1, 0), (2, 0, HALF))),
+        [whole, whole],
     )
-    chain_a = lax.ppermute(far_a, "ch", UP)
-    chain_b = lax.ppermute(far_b, "ch", DOWN)
-    direct_a = lax.ppermute(prev_a, "ch", DOWN)
-    direct_b = lax.ppermute(next_b, "ch", UP)
+    from_low = lax.ppermute(going_up, "ch", UP)
+    from_high = lax.ppermute(going_down, "ch", DOWN)
     next_a, prev_b, own_a, own_b = late_degrid(
-        arrived, (table1, table3, table0), (((0, 0), (2, 2)), ((1, 1), (2, 3))), away
+        arrived, (table1, table3, table0), (((0, 0, 0), (2, 2, 0)), ((1, 1, 0), (2, 3, 0))), [half, half, away, away]
     )
     ohq, ohp, opt, vis_re, vis_im, kept_b = make_setup(arrived, order_row, own_row)
-    legs = last_legs(chain_a, chain_b, direct_a, direct_b, next_a, prev_b)
+    chain_a, chain_b, *_ = last_legs(from_low, from_high, None, None, next_a, prev_b)
     model_a = exchange(model_a.reshape(64, 16, 256)).reshape(1024, 256)
 
     for step in range(ITERS):
         if step == 0:
-            parts = (in_hbm(own_a), in_hbm(own_b), *legs, in_hbm(kept_b))
-            mid, model_b = iterate((model_a, *parts, opt, in_hbm(vis_re), in_hbm(vis_im)), True)
+            sources = map(in_hbm, (vis_re, vis_im, kept_b, own_a, own_b, from_low, from_high))
+            mid, model_b = iterate((model_a, chain_a, chain_b, opt, *sources), True)
         else:
             rows = (model_a, model_b, opt, vis_re, vis_im, ohq, ohp)
-            (mid,) = iterate(rows + (everyone.reshape(S, 256), gains), False)
+            both = (everyone.reshape(S // 2, 256), others.reshape(S // 2, 256))
+            (mid,) = iterate(rows + both + (gains,), False)
         low = lax.ppermute(mid, "ch", UP)
         high = lax.ppermute(mid, "ch", DOWN)
         if step + 1 < ITERS:
             gains, block = smooth(where, mid, low, high, True)
             everyone = lax.all_to_all(block, ("y", "z"), split_axis=0, concat_axis=0, tiled=True)
-            everyone = lax.all_gather(everyone, "core", axis=0, tiled=True)
+            others = lax.ppermute(everyone, "core", [(0, 1), (1, 0)])
         else:
             (gains,) = smooth(where, mid, low, high, False)
     return gains.reshape(8, 2, ND, 16).transpose(3, 2, 1, 0).reshape(16, 2 * ND, 8)

time: 171 us -> 175 us (1.023)
  blocking collectives: 59.5 us -> 43.5 us
  starting transfers between devices: 45.3 us -> 56.2 us
  waiting for transfers between devices: 23.3 us -> 32.1 us
    all_gather x3 -> x0, blocking collectives: 16.1 us -> none  [body(): everyone = lax.all_gather(everyone, 'core', axis=0, tiled=True)]
    ppermute x0 -> x5, starting transfers between devices: none -> 13.9 us  [the longest x3 11.1 us: body(): others = lax.ppermute(everyone, 'core', [(0, 1), (1, 0)])]
    ppermute x0 -> x5, waiting for transfers between devices: none -> 11 us  [the longest x1 8.07 us: body(): from_low = lax.ppermute(going_up, 'ch', UP)]
    ppermute x2 -> x1, starting transfers between devices: 4.13 us -> 1.46 us  [body(): chain_b = lax.ppermute(far_b, 'ch', DOWN)]
    ppermute x2, waiting for transfers between devices: 7.58 us -> 5.62 us  [last_legs(): chain_a = lax.ppermute(pair_sum(chain_a, next_a), 'ch', UP)]
  transfers between devices with their start and end apart: 22 -> 23, of which waited for: 14 -> 16; matrix products, arithmetic and copies ran while one was open for 0% -> 0% of each run, Pallas kernels for 13% -> 12%
where the time goes in v3:
time: 175 us
  starting transfers between devices  56.2 us (32%)
  blocking collectives  43.5 us (25%)
  Pallas kernels  39.1 us (22%)
  waiting for transfers between devices  32.1 us (18%)
  local copies, waits for them, and re-layouts  3.56 us (2%)
    all_to_all x3, blocking collectives, body(): lax.all_to_all(block, ('y', 'z'), split_axis=0, concat_axis=0, tiled=True)  43.5 us
    all_to_all x2, starting transfers between devices, exchange(): return lax.all_to_all(value, BL, split_axis=0, concat_axis=0, tiled=True)  25.4 us
    pallas_call x4, Pallas kernels, iterate(): pl.pallas_call(iterate_kernel(first), out_shape=[jax.ShapeDtypeStruct((8,...  13.1 us
    ppermute x3, starting transfers between devices, body(): others = lax.ppermute(everyone, 'core', [(0, 1), (1, 0)])  11.1 us
    ppermute x1, waiting for transfers between devices, body(): from_low = lax.ppermute(going_up, 'ch', UP)  8.07 us
    pallas_call x2, Pallas kernels, degrid(): pl.pallas_call(degrid_kernel(count), out_shape=[half] * (2 * count) + [ta...  6.99 us
    ppermute x4, waiting for transfers between devices, body(): low = lax.ppermute(mid, 'ch', UP)  6.96 us
    pallas_call x2, Pallas kernels, late_degrid(): pl.pallas_call(late_kernel(jobs), out_shape=shapes, in_specs=[vmem, anywh...  6.85 us
  transfers between devices with their start and end apart: 23, of which 16 were waited for; matrix products, arithmetic and copies ran while one was open for 0% of the time, Pallas kernels for 12%

profile of v3, /device:TPU:1, one launch (start us, length us, event | category | flops | bytes accessed | tf_op | source)
XLA Modules:
  0.0 174.8 jit_solution(18360389366830704354)
XLA Ops:
  0.7 4.0 %payload.1 = (bf16[64,24,256]{2,1,0:T(8,128)(2,1)}, bf16[1024,128]{1,0:T(8,128)(2,1)S(1)}) custom-call(s32[4]{0:T(128)S(1)} %copy-done.4, bf16[16,2,2048]{2,1,0:T(2,128)(2,1)} %obs_ref.1, s32[16,2048]{1,0:T(8,128)} %flag_ref.1, s32[2,2048]{1,0:T(2,128)} %pair_ref.1, bf16[64,32,256]{2,1,0:T(8,128)(2,1)} %bitcast.35), custom_call_target="tpu_custom_call" | custom-call | tf_op jit(solution)/shard_map/payload/pallas_call | solution.py:180
  4.7 13.2 %all-to-all-start.1 = ((bf16[64,24,256]{2,1,0:T(8,128)(2,1)}), bf16[64,24,256]{2,1,0:T(8,128)(2,1)S(1)}, u32[]{:S(2)}, u32[]{:S(2)}) async-start(bf16[64,24,256]{2,1,0:T(8,128)(2,1)} %get-tuple-element.48), calls=%async_computation.1 | async-start | bytes 1572864 | tf_op jit(solution)/shard_map/all_to_all | solution.py:435
  17.9 2.9 %shard_map.74 = (bf16[512,256]{1,0:T(8,128)(2,1)S(1)}, bf16[512,256]{1,0:T(8,128)(2,1)S(1)}, bf16[256,1024]{1,0:T(8,128)(2,1)}) custom-call(s32[1]{0:T(128)} %bitcast.where_ref, s32[4]{0:T(128)S(1)} %copy-done.5, bf16[64,32,256]{2,1,0:T(8,128)(2,1)} %bitcast.36, bf16[4,64,16,256]{3,2,1,0:T(8,128)(2,1)} %refs_0_.3), custom_call_target="tpu_custom_call" | custom-call | tf_op jit(solution)/shard_map/pallas_call | solution.py:73
  20.8 1.2 collective-permute-start
  22.0 1.5 collective-permute-start.2
  23.5 4.1 %shard_map.73 = (bf16[512,256]{1,0:T(8,128)(2,1)S(1)}, bf16[512,256]{1,0:T(8,128)(2,1)S(1)}, bf16[512,256]{1,0:T(8,128)(2,1)S(1)}, bf16[512,256]{1,0:T(8,128)(2,...) custom-call(s32[1]{0:T(128)} %bitcast.where_ref, ...), custom_call_target="tpu_custom_call" | custom-call | tf_op jit(solution)/shard_map/pallas_call | solution.py:73
  27.6 1.3 collective-permute-start.4
  29.6 2.7 %collective-permute-start.3 = (bf16[512,256]{1,0:T(8,128)(2,1)S(1)}, bf16[512,256]{1,0:T(8,128)(2,1)S(1)}, u32[]{:S(2)}, u32[]{:S(2)}) collective-permute-start(bf16[512,256]{1,0:T(8,128)(2,1)S(1)} %pair.5), channel_id=1, source_target_pairs={{0,3},{1,0},{2,1},{3,2},{4,7},{5,4},{6,5},{7,6},{8,11},{9,8},{10,9... | collective-permute-start | bytes 786440 | tf_op jit(solution)/shard_map/ppermute | solution.py:430
  32.4 2.1 %collective-permute-done.4.near_a = bf16[512,256]{1,0:T(8,128)(2,1)S(1)} collective-permute-done((bf16[512,256]{1,0:T(8,128)(2,1)S(1)}, bf16[512,256]{1,0:T(8,128)(2,1)S(1)}, u32[]{:S(2)}, u32[]{:S(2)}) %collective-permute-start.4) | collective-permute-done | bytes 262176 | tf_op jit(solution)/shard_map/ppermute | solution.py:455
  34.5 2.1 %collective-permute-done.5.near_b = bf16[512,256]{1,0:T(8,128)(2,1)S(1)} collective-permute-done((bf16[512,256]{1,0:T(8,128)(2,1)S(1)}, bf16[512,256]{1,0:T(8,128)(2,1)S(1)}, u32[]{:S(2)}, u32[]{:S(2)}) %collective-permute-start.5) | collective-permute-done | bytes 262176 | tf_op jit(solution)/shard_map/ppermute | solution.py:456
  36.6 5.6 %collective-permute-done.1.chain_a = bf16[512,256]{1,0:T(8,128)(2,1)S(1)} collective-permute-done((bf16[512,256]{1,0:T(8,128)(2,1)S(1)}, bf16[512,256]{1,0:T(8,128)(2,1)S(1)}, u32[]{:S(2)}, u32[]{:S(2)}) %collective-permute-start.1) | collective-permute-done | bytes 262176 | tf_op jit(solution)/shard_map/ppermute | solution.py:429
  42.2 1.1 add.19
  43.3 12.2 %all-to-all-start = ((bf16[64,16,256]{2,1,0:T(8,128)(2,1)}), bf16[64,16,256]{2,1,0:T(8,128)(2,1)S(1)}, u32[]{:S(2)}, u32[]{:S(2)}) async-start(bf16[64,16,256]{2,1,0:T(8,128)(2,1)} %bitcast.2), calls=%async_computation | async-start | bytes 1048576 | tf_op jit(solution)/shard_map/all_to_all | solution.py:435
  55.5 3.5 %late.2 = (bf16[1024,256]{1,0:T(8,128)(2,1)}, bf16[1024,256]{1,0:T(8,128)(2,1)}) custom-call(bf16[64,24,256]{2,1,0:T(8,128)(2,1)S(1)} %all-to-all-done.1.pay_ref, bf16[256,1024]{1,0:T(8,128)(2,1)} %get-tuple-element.49.first_ref, bf16[256,1024]{1,0:T(8,128)(2,1)} %get-tuple-element.50.second_ref, bf16[256,1024]{1,0:T(8,128)(2,1)} %get-tuple-element.51.third_ref.first_ref), custom_call_target="tpu_custom_call" | custom-call | tf_op jit(solution)/shard_map/late/pallas_call | solution.py:129
  59.1 2.7 %collective-permute-start.8 = (bf16[1024,256]{1,0:T(8,128)(2,1)}, bf16[1024,256]{1,0:T(8,128)(2,1)S(1)}, u32[]{:S(2)}, u32[]{:S(2)}) collective-permute-start(bf16[1024,256]{1,0:T(8,128)(2,1)} %get-tuple-element.55), channel_id=1, source_target_pairs={{0,3},{1,0},{2,1},{3,2},{4,7},{5,4},{6,5},{7,6},{8,11},{9,8},{10,9... | collective-permute-start | bytes 1572872 | tf_op jit(solution)/shard_map/ppermute | solution.py:470
  62.1 3.4 %late.3 = (bf16[512,256]{1,0:T(8,128)(2,1)S(1)}, bf16[512,256]{1,0:T(8,128)(2,1)S(1)}, bf16[512,256]{1,0:T(8,128)(2,1)}, bf16[512,256]{1,0:T(8,128)(2,1)}) custom-call(bf16[64,24,256]{2,1,0:T(8,128)(2,1)S(1)} %all-to-all-done.1.pay_ref, bf16[256,1024]{1,0:T(8,128)(2,1)} %get-tuple-element.51.third_ref.first_ref, ...), custom_call_target="tpu_custom_call" | custom-call | tf_op jit(solution)/shard_map/late/pallas_call | solution.py:129
  65.5 8.1 %collective-permute-done.6.left_ref.refs_9_ = bf16[1024,256]{1,0:T(8,128)(2,1)S(1)} collective-permute-done((bf16[1024,256]{1,0:T(8,128)(2,1)}, bf16[1024,256]{1,0:T(8,128)(2,1)S(1)}, u32[]{:S(2)}, u32[]{:S(2)}) %collective-permute-start.6) | collective-permute-done | bytes 524320 | tf_op jit(solution)/shard_map/ppermute | solution.py:469
  73.6 0.8 copy-done.6
  74.4 1.0 pair.6
  75.5 0.8 copy-done.7
  76.3 1.0 pair.7
  77.3 2.7 %collective-permute-start.9 = (bf16[512,256]{1,0:T(8,128)(2,1)S(1)}, bf16[512,256]{1,0:T(8,128)(2,1)S(1)}, u32[]{:S(2)}, u32[]{:S(2)}) collective-permute-start(bf16[512,256]{1,0:T(8,128)(2,1)S(1)} %pair.7), channel_id=1, source_target_pairs={{0,3},{1,0},{2,1},{3,2},{4,7},{5,4},{6,5},{7,6},{8,11},{9,8},{10,9... | collective-permute-start | bytes 786440 | tf_op jit(solution)/shard_map/ppermute | solution.py:430
  80.2 4.7 %setup.1 = (bf16[2048,512]{1,0:T(8,128)(2,1)}, bf16[2048,128]{1,0:T(8,128)(2,1)}, bf16[16,2048]{1,0:T(8,128)(2,1)S(1)}, bf16[2048,128]{1,0:T(8,128)(2,1)}, bf16[...) custom-call(bf16[64,24,256]{2,1,0:T(8,128)(2,1)S(1)} %all-to-all-done.1.pay_ref, f32[1,512]{1,0:T(1,128)S(1)} %bitcast.34, ...), custom_call_target="tpu_custom_call" | custom-call | tf_op jit(solution)/shard_map/setup/pallas_call | solution.py:245
  84.9 4.3 %iterate0.1 = (f32[8,256]{1,0:T(8,128)S(1)}, bf16[1024,256]{1,0:T(8,128)(2,1)S(1)}) custom-call(bf16[1024,256]{1,0:T(8,128)(2,1)S(1)} %bitcast.24, bf16[512,256]{1,0:T(8,128)(2,1)S(1)} %collective-permute-done.7.refs_1_, bf16[512,256]{1,0:T(8,128)(2,1)S(1)} %collective-permute-done.9.refs_2_, bf16[16,2048]{1,0:T(8,128)(2,1)S(1)} %get-tuple-element.57.refs_3_.refs_2_, ...), custom_call_target="tpu_custom_call" | custom-call | tf_op jit(solution)/shard_map/iterate0/pallas_call | solution.py:342
  89.2 2.7 %collective-permute-start.11 = (f32[8,256]{1,0:T(8,128)S(1)}, f32[8,256]{1,0:T(8,128)S(1)}, u32[]{:S(2)}, u32[]{:S(2)}) collective-permute-start(f32[8,256]{1,0:T(8,128)S(1)} %get-tuple-element.66.mid_ref), channel_id=1, source_target_pairs={{0,3},{1,0},{2,1},{3,2},{4,7},{5,4},{6,5},{7,6},{8,11},{9,8},{10,9... | collective-permute-start | bytes 24584 | tf_op jit(solution)/shard_map/ppermute | solution.py:487
  91.9 0.8 collective-permute-done.11.high_ref
  92.7 2.9 %collective-permute-done.10.low_ref = f32[8,256]{1,0:T(8,128)S(1)} collective-permute-done((f32[8,256]{1,0:T(8,128)S(1)}, f32[8,256]{1,0:T(8,128)S(1)}, u32[]{:S(2)}, u32[]{:S(2)}) %collective-permute-start.10) | collective-permute-done | bytes 8224 | tf_op jit(solution)/shard_map/ppermute | solution.py:486
  95.7 18.6 %all_to_all.25 = bf16[32,8,256]{2,1,0:T(8,128)(2,1)S(1)} all-to-all(bf16[32,8,256]{2,1,0:T(8,128)(2,1)S(1)} %get-tuple-element.67), channel_id=1, replica_groups=mesh['y'=4,'z'=8,'core'=2,'ch'=4] {'y','z'}, dimensions={0} | all-to-all | bytes 262144 | tf_op jit(solution)/shard_map/all_to_all | solution.py:490
  114.3 5.2 %collective-permute-start.12 = (bf16[32,8,256]{2,1,0:T(8,128)(2,1)S(1)}, bf16[32,8,256]{2,1,0:T(8,128)(2,1)S(1)}, u32[]{:S(2)}, u32[]{:S(2)}) collective-permute-start(bf16[32,8,256]{2,1,0:T(8,128)(2,1)S(1)} %all_to_all.25), channel_id=1, source_target_pairs={{0,4},{4,0},{1,5},{5,1},{2,6},{6,2},{3,7},{7,3},{8,12},{12,8},{9,1... | collective-permute-start | bytes 393224 | tf_op jit(solution)/shard_map/ppermute | solution.py:491
  119.5 1.0 collective-permute-done.12
  120.5 2.9 %iterate.3.mid_ref = f32[8,256]{1,0:T(8,128)S(1)} custom-call(bf16[1024,256]{1,0:T(8,128)(2,1)S(1)} %bitcast.25, bf16[1024,256]{1,0:T(8,128)(2,1)S(1)} %get-tuple-element.63.refs_1_, bf16[16,2048]{1,0:T(8,128)(2,1)S(1)} %get-tuple-element.57.refs_3_.refs_2_, bf16[2048,128]{1,0:T(8,128)(2,1)S(1)} %copy-done.1, bf16[2048,128]{1,0:T(8,128)(2,1)S(1)} %copy-done.2, ...), custom_call_target="tpu_custom_call" | custom-call | tf_op jit(solution)/shard_map/iterate/pallas_call | solution.py:342
  123.4 1.5 collective-permute-start.13
  124.9 1.0 collective-permute-done.14.high_ref
  126.0 1.5 collective-permute-done.13.low_ref
  127.5 12.5 %all_to_all.26 = bf16[32,8,256]{2,1,0:T(8,128)(2,1)S(1)} all-to-all(bf16[32,8,256]{2,1,0:T(8,128)(2,1)S(1)} %get-tuple-element.69), channel_id=1, replica_groups=mesh['y'=4,'z'=8,'core'=2,'ch'=4] {'y','z'}, dimensions={0} | all-to-all | bytes 262144 | tf_op jit(solution)/shard_map/all_to_all | solution.py:490
  140.1 2.9 %collective-permute-start.15 = (bf16[32,8,256]{2,1,0:T(8,128)(2,1)S(1)}, bf16[32,8,256]{2,1,0:T(8,128)(2,1)S(1)}, u32[]{:S(2)}, u32[]{:S(2)}) collective-permute-start(bf16[32,8,256]{2,1,0:T(8,128)(2,1)S(1)} %all_to_all.26), channel_id=1, source_target_pairs={{0,4},{4,0},{1,5},{5,1},{2,6},{6,2},{3,7},{7,3},{8,12},{12,8},{9,1... | collective-permute-start | bytes 393224 | tf_op jit(solution)/shard_map/ppermute | solution.py:491
  143.0 1.0 collective-permute-done.15
  144.0 2.9 %iterate.4.mid_ref = f32[8,256]{1,0:T(8,128)S(1)} custom-call(bf16[1024,256]{1,0:T(8,128)(2,1)S(1)} %bitcast.26, bf16[1024,256]{1,0:T(8,128)(2,1)S(1)} %get-tuple-element.63.refs_1_, bf16[16,2048]{1,0:T(8,128)(2,1)S(1)} %get-tuple-element.57.refs_3_.refs_2_, bf16[2048,128]{1,0:T(8,128)(2,1)S(1)} %copy-done.1, bf16[2048,128]{1,0:T(8,128)(2,1)S(1)} %copy-done.2, ...), custom_call_target="tpu_custom_call" | custom-call | tf_op jit(solution)/shard_map/iterate/pallas_call | solution.py:342
  146.9 1.5 collective-permute-start.16
  148.4 1.0 collective-permute-done.17.high_ref
  149.5 1.3 collective-permute-done.16.low_ref
  150.8 12.4 %all_to_all.27 = bf16[32,8,256]{2,1,0:T(8,128)(2,1)S(1)} all-to-all(bf16[32,8,256]{2,1,0:T(8,128)(2,1)S(1)} %get-tuple-element.71), channel_id=1, replica_groups=mesh['y'=4,'z'=8,'core'=2,'ch'=4] {'y','z'}, dimensions={0} | all-to-all | bytes 262144 | tf_op jit(solution)/shard_map/all_to_all | solution.py:490
  163.2 2.9 %collective-permute-start.18 = (bf16[32,8,256]{2,1,0:T(8,128)(2,1)S(1)}, bf16[32,8,256]{2,1,0:T(8,128)(2,1)S(1)}, u32[]{:S(2)}, u32[]{:S(2)}) collective-permute-start(bf16[32,8,256]{2,1,0:T(8,128)(2,1)S(1)} %all_to_all.27), channel_id=1, source_target_pairs={{0,4},{4,0},{1,5},{5,1},{2,6},{6,2},{3,7},{7,3},{8,12},{12,8},{9,1... | collective-permute-start | bytes 393224 | tf_op jit(solution)/shard_map/ppermute | solution.py:491
  166.2 1.0 collective-permute-done.18
  167.2 2.9 %iterate.5.mid_ref = f32[8,256]{1,0:T(8,128)S(1)} custom-call(bf16[1024,256]{1,0:T(8,128)(2,1)S(1)} %bitcast.27, bf16[1024,256]{1,0:T(8,128)(2,1)S(1)} %get-tuple-element.63.refs_1_, bf16[16,2048]{1,0:T(8,128)(2,1)S(1)} %get-tuple-element.57.refs_3_.refs_2_, bf16[2048,128]{1,0:T(8,128)(2,1)S(1)} %copy-done.1, bf16[2048,128]{1,0:T(8,128)(2,1)S(1)} %copy-done.2, ...), custom_call_target="tpu_custom_call" | custom-call | tf_op jit(solution)/shard_map/iterate/pallas_call | solution.py:342
  170.1 1.5 collective-permute-start.19
  171.6 1.0 collective-permute-done.20.high_ref
  172.6 1.3 collective-permute-done.19.low_ref
  (51 shorter events, 3.3 us)
Async XLA Ops:
  0.0 17.9 %copy-start.5 = (s32[4]{0:T(128)S(1)}, s32[4]{0:T(128)}, u32[]{:S(2)}) copy-start(s32[4]{0:T(128)} %tile_ref.5) | copy-start | bytes 52
  0.0 0.7 copy-start.4
  4.7 38.6 %all-to-all-start.1 = ((bf16[64,24,256]{2,1,0:T(8,128)(2,1)}), bf16[64,24,256]{2,1,0:T(8,128)(2,1)S(1)}, u32[]{:S(2)}, u32[]{:S(2)}) async-start(bf16[64,24,256]{2,1,0:T(8,128)(2,1)} %get-tuple-element.48), calls=%async_computation.1 | async-start | bytes 1572864 | tf_op jit(solution)/shard_map/all_to_all | solution.py:435
  20.8 8.6 %collective-permute-start = (bf16[512,256]{1,0:T(8,128)(2,1)S(1)}, bf16[512,256]{1,0:T(8,128)(2,1)S(1)}, u32[]{:S(2)}, u32[]{:S(2)}) collective-permute-start(bf16[512,256]{1,0:T(8,128)(2,1)S(1)} %get-tuple-element.41), channel_id=1, source_target_pairs={{0,1},{1,2},{2,3},{3,0},{4,5},{5,6},{6,7},{7,4},{8,9},{9,10},{10,1... | collective-permute-start | bytes 786440 | tf_op jit(solution)/shard_map/ppermute | solution.py:450
  22.0 7.6 %collective-permute-start.2 = (bf16[512,256]{1,0:T(8,128)(2,1)S(1)}, bf16[512,256]{1,0:T(8,128)(2,1)S(1)}, u32[]{:S(2)}, u32[]{:S(2)}) collective-permute-start(bf16[512,256]{1,0:T(8,128)(2,1)S(1)} %get-tuple-element.43), channel_id=1, source_target_pairs={{0,3},{1,0},{2,1},{3,2},{4,7},{5,4},{6,5},{7,6},{8,11},{9,8},{10,9... | collective-permute-start | bytes 786440 | tf_op jit(solution)/shard_map/ppermute | solution.py:451
  27.6 7.0 %collective-permute-start.4 = (bf16[512,256]{1,0:T(8,128)(2,1)S(1)}, bf16[512,256]{1,0:T(8,128)(2,1)S(1)}, u32[]{:S(2)}, u32[]{:S(2)}) collective-permute-start(bf16[512,256]{1,0:T(8,128)(2,1)S(1)} %get-tuple-element.45), channel_id=1, source_target_pairs={{0,3},{1,0},{2,1},{3,2},{4,7},{5,4},{6,5},{7,6},{8,11},{9,8},{10,9... | collective-permute-start | bytes 786440 | tf_op jit(solution)/shard_map/ppermute | solution.py:455
  28.8 7.8 %collective-permute-start.5 = (bf16[512,256]{1,0:T(8,128)(2,1)S(1)}, bf16[512,256]{1,0:T(8,128)(2,1)S(1)}, u32[]{:S(2)}, u32[]{:S(2)}) collective-permute-start(bf16[512,256]{1,0:T(8,128)(2,1)S(1)} %get-tuple-element.46), channel_id=1, source_target_pairs={{0,1},{1,2},{2,3},{3,0},{4,5},{5,6},{6,7},{7,4},{8,9},{9,10},{10,1... | collective-permute-start | bytes 786440 | tf_op jit(solution)/shard_map/ppermute | solution.py:456
  29.5 12.8 %collective-permute-start.1 = (bf16[512,256]{1,0:T(8,128)(2,1)S(1)}, bf16[512,256]{1,0:T(8,128)(2,1)S(1)}, u32[]{:S(2)}, u32[]{:S(2)}) collective-permute-start(bf16[512,256]{1,0:T(8,128)(2,1)S(1)} %pair.4), channel_id=1, source_target_pairs={{0,1},{1,2},{2,3},{3,0},{4,5},{5,6},{6,7},{7,4},{8,9},{9,10},{10,1... | collective-permute-start | bytes 786440 | tf_op jit(solution)/shard_map/ppermute | solution.py:429
  29.6 12.6 %collective-permute-start.3 = (bf16[512,256]{1,0:T(8,128)(2,1)S(1)}, bf16[512,256]{1,0:T(8,128)(2,1)S(1)}, u32[]{:S(2)}, u32[]{:S(2)}) collective-permute-start(bf16[512,256]{1,0:T(8,128)(2,1)S(1)} %pair.5), channel_id=1, source_target_pairs={{0,3},{1,0},{2,1},{3,2},{4,7},{5,4},{6,5},{7,6},{8,11},{9,8},{10,9... | collective-permute-start | bytes 786440 | tf_op jit(solution)/shard_map/ppermute | solution.py:430
  43.3 18.5 %copy-start.8 = (s32[512]{0:T(512)S(1)}, s32[512]{0:T(512)}, u32[]{:S(2)}) copy-start(s32[512]{0:T(512)} %param.13) | copy-start | bytes 6148
  43.3 41.6 %all-to-all-start = ((bf16[64,16,256]{2,1,0:T(8,128)(2,1)}), bf16[64,16,256]{2,1,0:T(8,128)(2,1)S(1)}, u32[]{:S(2)}, u32[]{:S(2)}) async-start(bf16[64,16,256]{2,1,0:T(8,128)(2,1)} %bitcast.2), calls=%async_computation | async-start | bytes 1048576 | tf_op jit(solution)/shard_map/all_to_all | solution.py:435
  59.0 14.5 %collective-permute-start.6 = (bf16[1024,256]{1,0:T(8,128)(2,1)}, bf16[1024,256]{1,0:T(8,128)(2,1)S(1)}, u32[]{:S(2)}, u32[]{:S(2)}) collective-permute-start(bf16[1024,256]{1,0:T(8,128)(2,1)} %get-tuple-element.52), channel_id=1, source_target_pairs={{0,1},{1,2},{2,3},{3,0},{4,5},{5,6},{6,7},{7,4},{8,9},{9,10},{10,1... | collective-permute-start | bytes 1572872 | tf_op jit(solution)/shard_map/ppermute | solution.py:469
  59.1 16.4 %collective-permute-start.8 = (bf16[1024,256]{1,0:T(8,128)(2,1)}, bf16[1024,256]{1,0:T(8,128)(2,1)S(1)}, u32[]{:S(2)}, u32[]{:S(2)}) collective-permute-start(bf16[1024,256]{1,0:T(8,128)(2,1)} %get-tuple-element.55), channel_id=1, source_target_pairs={{0,3},{1,0},{2,1},{3,2},{4,7},{5,4},{6,5},{7,6},{8,11},{9,8},{10,9... | collective-permute-start | bytes 1572872 | tf_op jit(solution)/shard_map/ppermute | solution.py:470
  73.6 0.8 copy-start.6
  75.4 9.5 %collective-permute-start.7 = (bf16[512,256]{1,0:T(8,128)(2,1)S(1)}, bf16[512,256]{1,0:T(8,128)(2,1)S(1)}, u32[]{:S(2)}, u32[]{:S(2)}) collective-permute-start(bf16[512,256]{1,0:T(8,128)(2,1)S(1)} %pair.6), channel_id=1, source_target_pairs={{0,1},{1,2},{2,3},{3,0},{4,5},{5,6},{6,7},{7,4},{8,9},{9,10},{10,1... | collective-permute-start | bytes 786440 | tf_op jit(solution)/shard_map/ppermute | solution.py:429
  75.5 0.8 copy-start.7
  77.3 7.6 %collective-permute-start.9 = (bf16[512,256]{1,0:T(8,128)(2,1)S(1)}, bf16[512,256]{1,0:T(8,128)(2,1)S(1)}, u32[]{:S(2)}, u32[]{:S(2)}) collective-permute-start(bf16[512,256]{1,0:T(8,128)(2,1)S(1)} %pair.7), channel_id=1, source_target_pairs={{0,3},{1,0},{2,1},{3,2},{4,7},{5,4},{6,5},{7,6},{8,11},{9,8},{10,9... | collective-permute-start | bytes 786440 | tf_op jit(solution)/shard_map/ppermute | solution.py:430
  84.9 35.6 %copy-start = (bf16[2048,512]{1,0:T(8,128)(2,1)S(1)}, bf16[2048,512]{1,0:T(8,128)(2,1)}, u32[]{:S(2)}) copy-start(bf16[2048,512]{1,0:T(8,128)(2,1)} %get-tuple-element.64.refs_5_) | copy-start | bytes 6291460
  84.9 35.6 %copy-start.1 = (bf16[2048,128]{1,0:T(8,128)(2,1)S(1)}, bf16[2048,128]{1,0:T(8,128)(2,1)}, u32[]{:S(2)}) copy-start(bf16[2048,128]{1,0:T(8,128)(2,1)} %get-tuple-element.58.refs_4_.refs_3_) | copy-start | bytes 1572868
  84.9 35.6 %copy-start.2 = (bf16[2048,128]{1,0:T(8,128)(2,1)S(1)}, bf16[2048,128]{1,0:T(8,128)(2,1)}, u32[]{:S(2)}) copy-start(bf16[2048,128]{1,0:T(8,128)(2,1)} %get-tuple-element.59.refs_5_.refs_4_) | copy-start | bytes 1572868
  84.9 35.6 %copy-start.3 = (bf16[2048,128]{1,0:T(8,128)(2,1)S(1)}, bf16[2048,128]{1,0:T(8,128)(2,1)}, u32[]{:S(2)}) copy-start(bf16[2048,128]{1,0:T(8,128)(2,1)} %get-tuple-element.65.refs_6_) | copy-start | bytes 1572868
  89.2 3.5 %collective-permute-start.11 = (f32[8,256]{1,0:T(8,128)S(1)}, f32[8,256]{1,0:T(8,128)S(1)}, u32[]{:S(2)}, u32[]{:S(2)}) collective-permute-start(f32[8,256]{1,0:T(8,128)S(1)} %get-tuple-element.66.mid_ref), channel_id=1, source_target_pairs={{0,3},{1,0},{2,1},{3,2},{4,7},{5,4},{6,5},{7,6},{8,11},{9,8},{10,9... | collective-permute-start | bytes 24584 | tf_op jit(solution)/shard_map/ppermute | solution.py:487
  91.9 3.7 %collective-permute-start.10 = (f32[8,256]{1,0:T(8,128)S(1)}, f32[8,256]{1,0:T(8,128)S(1)}, u32[]{:S(2)}, u32[]{:S(2)}) collective-permute-start(f32[8,256]{1,0:T(8,128)S(1)} %get-tuple-element.66.mid_ref), channel_id=1, source_target_pairs={{0,1},{1,2},{2,3},{3,0},{4,5},{5,6},{6,7},{7,4},{8,9},{9,10},{10,1... | collective-permute-start | bytes 24584 | tf_op jit(solution)/shard_map/ppermute | solution.py:486
  114.3 6.2 %collective-permute-start.12 = (bf16[32,8,256]{2,1,0:T(8,128)(2,1)S(1)}, bf16[32,8,256]{2,1,0:T(8,128)(2,1)S(1)}, u32[]{:S(2)}, u32[]{:S(2)}) collective-permute-start(bf16[32,8,256]{2,1,0:T(8,128)(2,1)S(1)} %all_to_all.25), channel_id=1, source_target_pairs={{0,4},{4,0},{1,5},{5,1},{2,6},{6,2},{3,7},{7,3},{8,12},{12,8},{9,1... | collective-permute-start | bytes 393224 | tf_op jit(solution)/shard_map/ppermute | solution.py:491
  123.4 2.5 %collective-permute-start.14 = (f32[8,256]{1,0:T(8,128)S(1)}, f32[8,256]{1,0:T(8,128)S(1)}, u32[]{:S(2)}, u32[]{:S(2)}) collective-permute-start(f32[8,256]{1,0:T(8,128)S(1)} %iterate.3.mid_ref), channel_id=1, source_target_pairs={{0,3},{1,0},{2,1},{3,2},{4,7},{5,4},{6,5},{7,6},{8,11},{9,8},{10,9... | collective-permute-start | bytes 24584 | tf_op jit(solution)/shard_map/ppermute | solution.py:487
  123.4 4.0 %collective-permute-start.13 = (f32[8,256]{1,0:T(8,128)S(1)}, f32[8,256]{1,0:T(8,128)S(1)}, u32[]{:S(2)}, u32[]{:S(2)}) collective-permute-start(f32[8,256]{1,0:T(8,128)S(1)} %iterate.3.mid_ref), channel_id=1, source_target_pairs={{0,1},{1,2},{2,3},{3,0},{4,5},{5,6},{6,7},{7,4},{8,9},{9,10},{10,1... | collective-permute-start | bytes 24584 | tf_op jit(solution)/shard_map/ppermute | solution.py:486
  140.1 3.9 %collective-permute-start.15 = (bf16[32,8,256]{2,1,0:T(8,128)(2,1)S(1)}, bf16[32,8,256]{2,1,0:T(8,128)(2,1)S(1)}, u32[]{:S(2)}, u32[]{:S(2)}) collective-permute-start(bf16[32,8,256]{2,1,0:T(8,128)(2,1)S(1)} %all_to_all.26), channel_id=1, source_target_pairs={{0,4},{4,0},{1,5},{5,1},{2,6},{6,2},{3,7},{7,3},{8,12},{12,8},{9,1... | collective-permute-start | bytes 393224 | tf_op jit(solution)/shard_map/ppermute | solution.py:491
  146.9 2.5 %collective-permute-start.17 = (f32[8,256]{1,0:T(8,128)S(1)}, f32[8,256]{1,0:T(8,128)S(1)}, u32[]{:S(2)}, u32[]{:S(2)}) collective-permute-start(f32[8,256]{1,0:T(8,128)S(1)} %iterate.4.mid_ref), channel_id=1, source_target_pairs={{0,3},{1,0},{2,1},{3,2},{4,7},{5,4},{6,5},{7,6},{8,11},{9,8},{10,9... | collective-permute-start | bytes 24584 | tf_op jit(solution)/shard_map/ppermute | solution.py:487
  146.9 3.8 %collective-permute-start.16 = (f32[8,256]{1,0:T(8,128)S(1)}, f32[8,256]{1,0:T(8,128)S(1)}, u32[]{:S(2)}, u32[]{:S(2)}) collective-permute-start(f32[8,256]{1,0:T(8,128)S(1)} %iterate.4.mid_ref), channel_id=1, source_target_pairs={{0,1},{1,2},{2,3},{3,0},{4,5},{5,6},{6,7},{7,4},{8,9},{9,10},{10,1... | collective-permute-start | bytes 24584 | tf_op jit(solution)/shard_map/ppermute | solution.py:486
  163.2 3.9 %collective-permute-start.18 = (bf16[32,8,256]{2,1,0:T(8,128)(2,1)S(1)}, bf16[32,8,256]{2,1,0:T(8,128)(2,1)S(1)}, u32[]{:S(2)}, u32[]{:S(2)}) collective-permute-start(bf16[32,8,256]{2,1,0:T(8,128)(2,1)S(1)} %all_to_all.27), channel_id=1, source_target_pairs={{0,4},{4,0},{1,5},{5,1},{2,6},{6,2},{3,7},{7,3},{8,12},{12,8},{9,1... | collective-permute-start | bytes 393224 | tf_op jit(solution)/shard_map/ppermute | solution.py:491
  170.1 2.5 %collective-permute-start.20 = (f32[8,256]{1,0:T(8,128)S(1)}, f32[8,256]{1,0:T(8,128)S(1)}, u32[]{:S(2)}, u32[]{:S(2)}) collective-permute-start(f32[8,256]{1,0:T(8,128)S(1)} %iterate.5.mid_ref), channel_id=1, source_target_pairs={{0,3},{1,0},{2,1},{3,2},{4,7},{5,4},{6,5},{7,6},{8,11},{9,8},{10,9... | collective-permute-start | bytes 24584 | tf_op jit(solution)/shard_map/ppermute | solution.py:487
  170.1 3.8 %collective-permute-start.19 = (f32[8,256]{1,0:T(8,128)S(1)}, f32[8,256]{1,0:T(8,128)S(1)}, u32[]{:S(2)}, u32[]{:S(2)}) collective-permute-start(f32[8,256]{1,0:T(8,128)S(1)} %iterate.5.mid_ref), channel_id=1, source_target_pairs={{0,1},{1,2},{2,3},{3,0},{4,5},{5,6},{6,7},{7,4},{8,9},{9,10},{10,1... | collective-permute-start | bytes 24584 | tf_op jit(solution)/shard_map/ppermute | solution.py:486
